TPU v7x, 32 devices: a whole 2x2x4 slice. The times are simulated.
32 devices in a mesh: blk: 4 (over z), batch: 8 (over y, x, core).
Axes of the slice: x: 2, y: 2, z: 4, core: 2. Of those that a mesh axis runs over, the one named last changes fastest.
Arguments:
- tokens: bfloat16 [24, 512, 768], P('batch', 'blk'), may hold values from -6 to 6
- segment_ids: int32 [24, 512], P('batch', 'blk'), may hold values from 0 to 3, never falling along the last dimension, each value on 1 to 384 neighbouring positions
- w_query: bfloat16 [768, 768], replicated, may hold values from -0.21875 to 0.21875
- b_query: float32 [768], replicated, may hold values from -3 to 3
- w_key: bfloat16 [768, 768], replicated, may hold values from -0.21875 to 0.21875
- w_value: bfloat16 [768, 768], replicated, may hold values from -0.21875 to 0.21875
- b_value: float32 [768], replicated, may hold values from -3 to 3
- w_out: bfloat16 [768, 768], replicated, may hold values from -1.25 to 1.25
- b_out: float32 [768], replicated, may hold values from -2 to 2
- gain_first: float32 [768], replicated, may hold values from 0.5 to 1.5
- shift_first: float32 [768], replicated, may hold values from -2 to 2
- w_inner: bfloat16 [768, 3072], replicated, may hold values from -0.21875 to 0.21875
- b_inner: float32 [3072], replicated, may hold values from -3 to 3
- w_outer: bfloat16 [3072, 768], replicated, may hold values from -0.109375 to 0.109375
- b_outer: float32 [768], replicated, may hold values from -2 to 2
- gain_second: float32 [768], replicated, may hold values from 0.5 to 1.5
- shift_second: float32 [768], replicated, may hold values from -2 to 2
- cotangent: bfloat16 [24, 512, 768], P('batch', 'blk'), may hold values from -6 to 6
Outputs:
- layer_out: bfloat16 [24, 512, 768], P('batch', 'blk')
- input_grad: bfloat16 [24, 512, 768], P('batch', 'blk')
- grad_w_query: float32 [768, 768], P('batch')
- grad_b_query: float32 [768], P('batch')
- grad_w_key: float32 [768, 768], P('batch')
- grad_w_value: float32 [768, 768], P('batch')
- grad_b_value: float32 [768], P('batch')
- grad_w_out: float32 [768, 768], P('batch')
- grad_b_out: float32 [768], P('batch')
- grad_gain_first: float32 [768], P('batch')
- grad_shift_first: float32 [768], P('batch')
- grad_w_inner: float32 [768, 3072], P('batch')
- grad_b_inner: float32 [3072], P('batch')
- grad_w_outer: float32 [3072, 768], P('batch')
- grad_b_outer: float32 [768], P('batch')
- grad_gain_second: float32 [768], P('batch')
- grad_shift_second: float32 [768], P('batch')
Inputs may be any that keep to these rules, and one draw needn't show every extreme that they name: `segment_ids`: within each row the numbers never fall, and no fragment has more than 384 tokens; some fragment has exactly that many.
All inputs are finite; a program needn't handle non-finite values.
Results may differ from a plain program's by a relative error of at most 0.019.
Values may be sent and summed in bfloat16 or wider, within the bound.
A program may use at most 128 MiB of HBM per device.

v0:
```python
import math

import jax
import jax.numpy as jnp
from jax import lax
from jax.sharding import PartitionSpec as P

HEADS = 12
HEAD_DIM = 64


epsilon = 1e-05


def matmul(left, right):
    return jnp.dot(left, right, preferred_element_type=jnp.float32)


def norm_forward(resid, gain, shift):
    center = resid - jnp.mean(resid, axis=-1, keepdims=True)
    inverse = lax.rsqrt(jnp.mean(center * center, axis=-1, keepdims=True) + epsilon)
    unit = center * inverse
    return (unit * gain + shift, unit, inverse)


def norm_backward(upstream, unit, inverse, gain):
    scaled = upstream * gain
    inner = inverse * (
        scaled
        - jnp.mean(scaled, axis=-1, keepdims=True)
        - unit * jnp.mean(scaled * unit, axis=-1, keepdims=True)
    )
    return (inner, jnp.sum(upstream * unit, axis=0), jnp.sum(upstream, axis=0))


def per_device(
    tokens,
    segment_ids,
    w_query,
    b_query,
    w_key,
    w_value,
    b_value,
    w_out,
    b_out,
    gain_first,
    shift_first,
    w_inner,
    b_inner,
    w_outer,
    b_outer,
    gain_second,
    shift_second,
    cotangent,
):
    seq_local, block_tokens, model_width = tokens.shape
    row_count = seq_local * block_tokens
    flat_in = tokens.reshape(row_count, model_width)
    resid_in = flat_in.astype(jnp.float32)
    head_shape = (seq_local, block_tokens, HEADS, HEAD_DIM)
    query = (matmul(flat_in, w_query) + b_query).astype(jnp.bfloat16).reshape(head_shape)
    keyed = matmul(flat_in, w_key).astype(jnp.bfloat16).reshape(head_shape)
    valued = (matmul(flat_in, w_value) + b_value).astype(jnp.bfloat16).reshape(head_shape)
    keys_row, values_row, segs_row = (
        lax.all_gather(keyed, "blk", axis=1, tiled=True),
        lax.all_gather(valued, "blk", axis=1, tiled=True),
        lax.all_gather(segment_ids, "blk", axis=1, tiled=True),
    )
    raw = jnp.einsum("sqhd,skhd->shqk", query, keys_row, preferred_element_type=jnp.float32) * 0.125
    same = segment_ids[:, None, :, None] == segs_row[:, None, None, :]
    score = jnp.where(same, raw, -1e30)
    top = jnp.max(score, axis=-1, keepdims=True)
    expo = jnp.exp(score - top)
    total = jnp.sum(expo, axis=-1, keepdims=True)
    prob = expo / total
    prob_low = prob.astype(jnp.bfloat16)
    attended = jnp.einsum(
        "shqk,skhd->sqhd", prob_low, values_row, preferred_element_type=jnp.float32
    )
    attended_low = attended.reshape(row_count, model_width).astype(jnp.bfloat16)
    first = resid_in + matmul(attended_low, w_out) + b_out
    normed, unit_first, inverse_first = norm_forward(first, gain_first, shift_first)
    normed_low = normed.astype(jnp.bfloat16)
    pre = matmul(normed_low, w_inner) + b_inner
    act_low = jax.nn.gelu(pre, approximate=False).astype(jnp.bfloat16)
    second = normed + matmul(act_low, w_outer) + b_outer
    result, unit_second, inverse_second = norm_forward(second, gain_second, shift_second)
    layer_out = result.astype(jnp.bfloat16).reshape(seq_local, block_tokens, model_width)
    upstream = cotangent.reshape(row_count, model_width).astype(jnp.float32)
    d_second, g_gain_second, g_shift_second = norm_backward(
        upstream, unit_second, inverse_second, gain_second
    )
    d_outer = d_second.astype(jnp.bfloat16)
    g_w_outer = jnp.einsum("tf,td->fd", act_low, d_outer, preferred_element_type=jnp.float32)
    g_b_outer = jnp.sum(d_outer.astype(jnp.float32), axis=0)
    d_act = jnp.einsum("td,fd->tf", d_outer, w_outer, preferred_element_type=jnp.float32)
    slope = 0.5 * (1.0 + lax.erf(pre * (1.0 / math.sqrt(2.0)))) + pre * jnp.exp(
        -0.5 * pre * pre
    ) * (1.0 / math.sqrt(2.0 * math.pi))
    d_pre = (d_act * slope).astype(jnp.bfloat16)
    g_w_inner = jnp.einsum("td,tf->df", normed_low, d_pre, preferred_element_type=jnp.float32)
    g_b_inner = jnp.sum(d_pre.astype(jnp.float32), axis=0)
    d_normed = d_second + jnp.einsum(
        "tf,df->td", d_pre, w_inner, preferred_element_type=jnp.float32
    )
    d_first, g_gain_first, g_shift_first = norm_backward(
        d_normed, unit_first, inverse_first, gain_first
    )
    d_branch = d_first.astype(jnp.bfloat16)
    g_w_out = jnp.einsum("td,te->de", attended_low, d_branch, preferred_element_type=jnp.float32)
    g_b_out = jnp.sum(d_branch.astype(jnp.float32), axis=0)
    d_attended = jnp.einsum("te,de->td", d_branch, w_out, preferred_element_type=jnp.float32)
    d_attended = d_attended.astype(jnp.bfloat16).reshape(head_shape)
    keys_back, values_back = (keys_row, values_row)
    prob_back, prob_back_low = (prob, prob_low)
    d_prob = jnp.einsum(
        "sqhd,skhd->shqk", d_attended, values_back, preferred_element_type=jnp.float32
    )
    centre = jnp.sum(d_prob * prob_back, axis=-1, keepdims=True)
    d_score = (prob_back * (d_prob - centre)).astype(jnp.bfloat16)
    d_query = (
        jnp.einsum("shqk,skhd->sqhd", d_score, keys_back, preferred_element_type=jnp.float32)
        * 0.125
    ).astype(jnp.bfloat16)
    d_keys_row = (
        jnp.einsum("shqk,sqhd->skhd", d_score, query, preferred_element_type=jnp.float32) * 0.125
    )
    d_values_row = jnp.einsum(
        "shqk,sqhd->skhd", prob_back_low, d_attended, preferred_element_type=jnp.float32
    )
    d_keyed, d_valued = (
        lax.psum_scatter(
            d_keys_row.astype(jnp.bfloat16), "blk", scatter_dimension=1, tiled=True
        ).astype(jnp.float32),
        lax.psum_scatter(
            d_values_row.astype(jnp.bfloat16), "blk", scatter_dimension=1, tiled=True
        ).astype(jnp.float32),
    )
    d_query = d_query.reshape(row_count, model_width)
    d_keyed = d_keyed.astype(jnp.bfloat16).reshape(row_count, model_width)
    d_valued = d_valued.astype(jnp.bfloat16).reshape(row_count, model_width)
    g_w_query = jnp.einsum("td,te->de", flat_in, d_query, preferred_element_type=jnp.float32)
    g_b_query = jnp.sum(d_query.astype(jnp.float32), axis=0)
    g_w_key = jnp.einsum("td,te->de", flat_in, d_keyed, preferred_element_type=jnp.float32)
    g_w_value = jnp.einsum("td,te->de", flat_in, d_valued, preferred_element_type=jnp.float32)
    g_b_value = jnp.sum(d_valued.astype(jnp.float32), axis=0)
    d_input = d_first + jnp.einsum(
        "te,de->td", d_query, w_query, preferred_element_type=jnp.float32
    )
    d_input = d_input + jnp.einsum("te,de->td", d_keyed, w_key, preferred_element_type=jnp.float32)
    d_input = d_input + jnp.einsum(
        "te,de->td", d_valued, w_value, preferred_element_type=jnp.float32
    )
    input_grad = d_input.astype(jnp.bfloat16).reshape(seq_local, block_tokens, model_width)
    shares = (
        lax.psum_scatter(g_w_query, "batch", scatter_dimension=0, tiled=True),
        lax.psum_scatter(g_b_query, "batch", scatter_dimension=0, tiled=True),
        lax.psum_scatter(g_w_key, "batch", scatter_dimension=0, tiled=True),
        lax.psum_scatter(g_w_value, "batch", scatter_dimension=0, tiled=True),
        lax.psum_scatter(g_b_value, "batch", scatter_dimension=0, tiled=True),
        lax.psum_scatter(g_w_out, "batch", scatter_dimension=0, tiled=True),
        lax.psum_scatter(g_b_out, "batch", scatter_dimension=0, tiled=True),
        lax.psum_scatter(g_gain_first, "batch", scatter_dimension=0, tiled=True),
        lax.psum_scatter(g_shift_first, "batch", scatter_dimension=0, tiled=True),
        lax.psum_scatter(g_w_inner, "batch", scatter_dimension=0, tiled=True),
        lax.psum_scatter(g_b_inner, "batch", scatter_dimension=0, tiled=True),
        lax.psum_scatter(g_w_outer, "batch", scatter_dimension=0, tiled=True),
        lax.psum_scatter(g_b_outer, "batch", scatter_dimension=0, tiled=True),
        lax.psum_scatter(g_gain_second, "batch", scatter_dimension=0, tiled=True),
        lax.psum_scatter(g_shift_second, "batch", scatter_dimension=0, tiled=True),
    )
    summed = (
        lax.psum(shares[0].astype(jnp.bfloat16), "blk").astype(jnp.float32),
        lax.psum(shares[1].astype(jnp.bfloat16), "blk").astype(jnp.float32),
        lax.psum(shares[2].astype(jnp.bfloat16), "blk").astype(jnp.float32),
        lax.psum(shares[3].astype(jnp.bfloat16), "blk").astype(jnp.float32),
        lax.psum(shares[4].astype(jnp.bfloat16), "blk").astype(jnp.float32),
        lax.psum(shares[5].astype(jnp.bfloat16), "blk").astype(jnp.float32),
        lax.psum(shares[6].astype(jnp.bfloat16), "blk").astype(jnp.float32),
        lax.psum(shares[7].astype(jnp.bfloat16), "blk").astype(jnp.float32),
        lax.psum(shares[8].astype(jnp.bfloat16), "blk").astype(jnp.float32),
        lax.psum(shares[9].astype(jnp.bfloat16), "blk").astype(jnp.float32),
        lax.psum(shares[10].astype(jnp.bfloat16), "blk").astype(jnp.float32),
        lax.psum(shares[11].astype(jnp.bfloat16), "blk").astype(jnp.float32),
        lax.psum(shares[12].astype(jnp.bfloat16), "blk").astype(jnp.float32),
        lax.psum(shares[13].astype(jnp.bfloat16), "blk").astype(jnp.float32),
        lax.psum(shares[14].astype(jnp.bfloat16), "blk").astype(jnp.float32),
    )
    return (
        layer_out,
        input_grad,
        summed[0],
        summed[1],
        summed[2],
        summed[3],
        summed[4],
        summed[5],
        summed[6],
        summed[7],
        summed[8],
        summed[9],
        summed[10],
        summed[11],
        summed[12],
        summed[13],
        summed[14],
    )


def solution(mesh):
    return jax.shard_map(
        per_device,
        mesh=mesh,
        in_specs=(
            P("batch", "blk", None),
            P("batch", "blk"),
            P(),
            P(),
            P(),
            P(),
            P(),
            P(),
            P(),
            P(),
            P(),
            P(),
            P(),
            P(),
            P(),
            P(),
            P(),
            P("batch", "blk", None),
        ),
        out_specs=(
            P("batch", "blk", None),
            P("batch", "blk", None),
            P("batch", None),
            P("batch"),
            P("batch", None),
            P("batch", None),
            P("batch"),
            P("batch", None),
            P("batch"),
            P("batch"),
            P("batch"),
            P("batch", None),
            P("batch"),
            P("batch", None),
            P("batch"),
            P("batch"),
            P("batch"),
        ),
        check_vma=False,
    )
```

profile of v0, /device:TPU:0, one launch (start us, length us, event | category | flops | bytes accessed | tf_op | source)
XLA Modules:
  0.0 727.1 jit_solution(642191611935414513)
XLA Ops:
  25.9 15.2 %all_gather.10 = s32[3,512]{1,0:T(4,128)S(1)} all-gather(s32[3,128]{1,0:T(4,128)S(1)} %copy-done.35), channel_id=1, replica_groups=mesh['blk'=4,'batch'=8] {'blk'}, dimensions={1}, use_global_device_ids=true | all-gather | bytes 7680 | tf_op jit(solution)/shard_map/all_gather | solution.py:67
  42.6 24.9 %all-gather.5.cloned.1.call-done = bf16[3,512,12,64]{1,3,2,0:T(8,128)(2,1)} async-done(((bf16[3,128,12,64]{1,3,2,0:T(8,128)(2,1)}), bf16[3,512,12,64]{1,3,2,0:T(8,128)(2,1)}) %all-gather.5.cloned.1.call-update) | async-done | bytes 2359312 | tf_op jit(solution)/shard_map/all_gather | solution.py:65
  67.5 8.7 %fusion.80 = (f32[3,12,128]{2,1,0:T(8,128)S(1)}, f32[3,12,128,512]{3,2,1,0:T(8,128)}) fusion(pred[3,128,512]{2,1,0:T(8,128)(4,1)S(1)} %broadcast_compare_fusion, bf16[3,128,12,64]{1,3,2,0:T(8,128)(2,1)S(1)} %copy.66, bf16[3,512,12,64]{1,3,2,0:T(8,128)(2,1)} %all-gather.5.cloned.1.call-done), kind=kOutput, calls=%fused_computation.138 | convolution fusion | flops 311427584 | bytes 12601344 | tf_op jit(solution)/shard_map/sub | solution.py:73
  76.2 42.2 %all-gather.3.cloned.1.call-done = bf16[3,512,12,64]{1,3,2,0:T(8,128)(2,1)} async-done(((bf16[3,128,12,64]{1,3,2,0:T(8,128)(2,1)}), bf16[3,512,12,64]{1,3,2,0:T(8,128)(2,1)}) %all-gather.3.cloned.1.call-update) | async-done | bytes 2359312 | tf_op jit(solution)/shard_map/all_gather | solution.py:66
  118.4 6.2 fusion.38
  126.4 14.0 %fusion.4 = (bf16[384,3072]{1,0:T(8,128)(2,1)S(1)}, f32[384,3072]{1,0:T(8,128)S(1)}) fusion(f32[3072]{0:T(1024)S(1)} %copy-done.40, bf16[768,3072]{1,0:T(8,128)(2,1)} %param.29, f32[384,768]{1,0:T(8,128)S(1)} %get-tuple-element.108, f32[768]{0:T(1024)S(1)} %copy-done.24, f32[768]{0:T(1024)S(1)} %copy-done.23, f32[384]{0:T(512)S(1)} %add_rsqrt_fusion.1, ...), kind=kOutput, calls=%fused_computation.10 | convolution fusion | flops 1891270656 | bytes 12997632 | tf_op jit(solution)/shard_map/dot_general | solution.py:16
  160.5 6.0 convert_bitcast_fusion
  166.5 8.4 %copy.84 = bf16[3,512,12,64]{3,2,0,1:T(8,128)(2,1)} copy(bf16[3,512,12,64]{1,3,2,0:T(8,128)(2,1)} %convert_bitcast_fusion) | data formatting | bytes 4718592
  174.9 8.4 %reshape.156 = bf16[512,2304]{1,0:T(8,128)(2,1)} reshape(bf16[512,3,12,64]{3,2,1,0:T(8,128)(2,1)} %bitcast.117) | data formatting | bytes 4718592
  183.3 5.7 multiply_reduce_fusion
  198.6 8.4 %copy.82 = bf16[3,512,12,64]{3,2,0,1:T(8,128)(2,1)} copy(bf16[3,512,12,64]{1,3,2,0:T(8,128)(2,1)} %fusion.21) | data formatting | bytes 4718592
  207.0 8.4 %reshape.154 = bf16[512,2304]{1,0:T(8,128)(2,1)} reshape(bf16[512,3,12,64]{3,2,1,0:T(8,128)(2,1)} %bitcast.118) | data formatting | bytes 4718592
  243.7 35.7 %reduce-scatter.25.cloned.1.call-done = bf16[128,2304]{1,0:T(8,128)(2,1)} async-done(((bf16[512,2304]{1,0:T(8,128)(2,1)}), bf16[128,2304]{1,0:T(8,128)(2,1)}) %reduce-scatter.25.cloned.1.call-update) | async-done | bytes 589840
  292.2 7.1 fusion.75
  300.6 8.0 %fusion.70 = f32[3072,768]{1,0:T(8,128)} fusion(bf16[384,3072]{1,0:T(8,128)(2,1)} %copy-done.13, f32[384,768]{1,0:T(8,128)S(1)} %copy-done.12), kind=kOutput, calls=%fused_computation.131 | convolution fusion | flops 1812234240 | bytes 12976128 | tf_op jit(solution)/shard_map/tf,td->fd/dot_general | solution.py:94
  308.8 15.8 %reduce-scatter.19.cloned.1.call-done = f32[96,768]{1,0:T(8,128)} async-done(((f32[768,768]{1,0:T(8,128)}), f32[96,768]{1,0:T(8,128)}) %reduce-scatter.19.cloned.1.call-update) | async-done | bytes 294928 | tf_op jit(solution)/shard_map/reduce_scatter | solution.py:161
  326.3 44.4 %reduce-scatter.29.cloned.1.call-done = f32[96,768]{1,0:T(8,128)} async-done(((f32[768,768]{1,0:T(8,128)}), f32[96,768]{1,0:T(8,128)}) %reduce-scatter.29.cloned.1.call-update) | async-done | bytes 294928
  372.5 44.1 %reduce-scatter.33.cloned.1.call-done = f32[96,768]{1,0:T(8,128)} async-done(((f32[768,768]{1,0:T(8,128)}), f32[96,768]{1,0:T(8,128)}) %reduce-scatter.33.cloned.1.call-update) | async-done | bytes 294928
  418.4 44.4 %reduce-scatter.31.cloned.1.call-done = f32[96,768]{1,0:T(8,128)} async-done(((f32[768,768]{1,0:T(8,128)}), f32[96,768]{1,0:T(8,128)}) %reduce-scatter.31.cloned.1.call-update) | async-done | bytes 294928
  464.6 78.2 %reduce-scatter.21.cloned.1.call-done = f32[96,3072]{1,0:T(8,128)} async-done(((f32[768,3072]{1,0:T(8,128)}), f32[96,3072]{1,0:T(8,128)}) %reduce-scatter.21.cloned.1.call-update) | async-done | bytes 1179664 | tf_op jit(solution)/shard_map/reduce_scatter | solution.py:165
  545.0 77.7 %reduce-scatter.23.cloned.1.call-done = f32[384,768]{1,0:T(8,128)} async-done(((f32[3072,768]{1,0:T(8,128)}), f32[384,768]{1,0:T(8,128)}) %reduce-scatter.23.cloned.1.call-update) | async-done | bytes 1179664 | tf_op jit(solution)/shard_map/reduce_scatter | solution.py:167
  631.5 25.1 %all-reduce.9 = (bf16[768]{0:T(1024)(128)(2,1)S(1)}, bf16[768]{0:T(1024)(128)(2,1)S(1)}, bf16[768]{0:T(1024)(128)(2,1)S(1)}, bf16[768]{0:T(1024)(128)(2,1)S(1)},...) all-reduce(f32[768]{0:T(1024)S(1)} %reduce_sum.186, ...), channel_id=5, replica_groups=mesh['blk'=4,'batch'=8] {'batch'}, use_global_device_ids=true, to_apply=%region_16.17.clone | all-reduce | flops 9216 | bytes 55296
  657.3 12.4 %all-reduce.10 = (bf16[96]{0:T(256)(128)(2,1)S(1)}, bf16[96]{0:T(256)(128)(2,1)S(1)}, bf16[96]{0:T(256)(128)(2,1)S(1)}, bf16[96]{0:T(256)(128)(2,1)S(1)}, bf16[9...) all-reduce(bf16[96]{0:T(256)(128)(2,1)S(1)} %dynamic-slice.35, ...), channel_id=1, replica_groups=mesh['blk'=4,'batch'=8] {'blk'}, use_global_device_ids=true, to_apply=%region_17.18 | all-reduce | flops 1152 | bytes 4608 | tf_op jit(solution)/shard_map/psum | solution.py:174
  678.0 32.0 %all-reduce.14.cloned.1.call-done = (bf16[96,768]{0,1:T(8,128)(2,1)}, bf16[96,768]{0,1:T(8,128)(2,1)}, bf16[96,768]{0,1:T(8,128)(2,1)}, bf16[96,768]{1,0:T(8,128...) async-done(((bf16[96,768]{0,1:T(8,128)(2,1)}, bf16[96,768]{0,1:T(8,128)(2,1)}, bf16[96,768]{0,1:T(8,128)(2,1)}, bf16[96,768]{1,0:T(8,128)(2,1)}, ...) | async-done | bytes 1769488 | tf_op jit(solution)/shard_map/psum | solution.py:173
  (209 shorter events, 129.4 us)
Async XLA Ops:
  7.2 118.0 %copy-start = (bf16[768,768]{1,0:T(8,128)(2,1)S(1)}, bf16[768,768]{1,0:T(8,128)(2,1)}, u32[]{:S(2)}) copy-start(bf16[768,768]{1,0:T(8,128)(2,1)} %param.25) | copy-start | bytes 3538948
  7.2 60.3 %all-gather.5.cloned.1.call-start = ((), (), s32[]{:S(2)}) async-start(), calls=%async_computation.9 | async-start | bytes 2949120 | tf_op jit(solution)/shard_map/all_gather | solution.py:65
  14.0 104.5 %all-gather.3.cloned.1.call-start = ((), (), s32[]{:S(2)}) async-start(), calls=%async_computation.8 | async-start | bytes 2949120 | tf_op jit(solution)/shard_map/all_gather | solution.py:66
  19.2 212.0 %reduce-scatter.27.cloned.1.call-start = ((), (), s32[]{:S(2)}) async-start(), calls=%async_computation.14 | async-start | bytes 2949120
  20.7 20.3 %copy-start.5 = (bf16[3,128,768]{2,1,0:T(8,128)(2,1)S(1)}, bf16[3,128,768]{2,1,0:T(8,128)(2,1)}, u32[]{:S(2)}) copy-start(bf16[3,128,768]{2,1,0:T(8,128)(2,1)} %param.35) | copy-start | bytes 1769476
  20.7 20.3 %copy-start.25 = (f32[768]{0:T(1024)S(1)}, f32[768]{0:T(1024)}, u32[]{:S(2)}) copy-start(f32[768]{0:T(1024)} %param.33) | copy-start | bytes 9220
  25.8 50.4 %copy-start.17 = (bf16[3,128,12,64]{1,3,2,0:T(8,128)(2,1)}, bf16[3,128,12,64]{1,3,2,0:T(8,128)(2,1)S(1)}, u32[]{:S(2)}) copy-start(bf16[3,128,12,64]{1,3,2,0:T(8,128)(2,1)S(1)} %copy.66) | copy-start | bytes 1769476
  76.2 48.5 %copy-start.28 = (f32[3,12,128]{2,1,0:T(8,128)}, f32[3,12,128]{2,1,0:T(8,128)S(1)}, u32[]{:S(2)}) copy-start(f32[3,12,128]{2,1,0:T(8,128)S(1)} %get-tuple-element.105) | copy-start | bytes 55300
  125.3 15.2 %slice-start = ((s8[4718592]{0:T(1024)(128)(4,1)}), s8[4194304]{0:T(1024)(128)(4,1)S(1)}, s32[]{:S(2)}) async-start(s8[4718592]{0:T(1024)(128)(4,1)} %bitcast.139), calls=%async_computation.19 | async-start | bytes 8388608
  126.4 14.1 %slice-start.1 = ((s8[4718592]{0:T(1024)(128)(4,1)}), s8[524288]{0:T(1024)(128)(4,1)S(1)}, s32[]{:S(2)}) async-start(s8[4718592]{0:T(1024)(128)(4,1)} %bitcast.139), calls=%async_computation.20 | async-start | bytes 1048576
  126.4 14.1 %copy-start.44 = (f32[768]{0:T(1024)S(1)}, f32[768]{0:T(1024)}, u32[]{:S(2)}) copy-start(f32[768]{0:T(1024)} %param.32) | copy-start | bytes 9220
  183.3 96.1 %reduce-scatter.25.cloned.1.call-start = ((), (), s32[]{:S(2)}) async-start(), calls=%async_computation.13 | async-start | bytes 2949120
  215.4 109.2 %reduce-scatter.19.cloned.1.call-start = ((), (), s32[]{:S(2)}) async-start(), calls=%async_computation.10 | async-start | bytes 2654208 | tf_op jit(solution)/shard_map/reduce_scatter | solution.py:161
  218.8 151.9 %reduce-scatter.29.cloned.1.call-start = ((), (), s32[]{:S(2)}) async-start(), calls=%async_computation.15 | async-start | bytes 2654208
  231.2 185.4 %reduce-scatter.33.cloned.1.call-start = ((), (), s32[]{:S(2)}) async-start(), calls=%async_computation.17 | async-start | bytes 2654208
  243.7 219.1 %reduce-scatter.31.cloned.1.call-start = ((), (), s32[]{:S(2)}) async-start(), calls=%async_computation.16 | async-start | bytes 2654208
  292.1 250.7 %reduce-scatter.21.cloned.1.call-start = ((), (), s32[]{:S(2)}) async-start(), calls=%async_computation.11 | async-start | bytes 10616832 | tf_op jit(solution)/shard_map/reduce_scatter | solution.py:165
  299.3 323.4 %reduce-scatter.23.cloned.1.call-start = ((), (), s32[]{:S(2)}) async-start(), calls=%async_computation.12 | async-start | bytes 10616832 | tf_op jit(solution)/shard_map/reduce_scatter | solution.py:167
  308.6 401.4 %all-reduce.14.cloned.1.call-start = ((), (), s32[]{:S(2)}) async-start(), calls=%async_computation.18 | async-start | bytes 3833856 | tf_op jit(solution)/shard_map/psum | solution.py:173
  464.6 160.3 %copy-start.45 = (u32[32]{0:T(128)S(1)}, u32[32]{0:T(128)}, u32[]{:S(2)}) copy-start(u32[32]{0:T(128)} %constant.90) | copy-start | bytes 388
  464.6 162.2 %copy-start.27 = (f32[12,64]{1,0:T(8,128)S(1)}, f32[12,64]{1,0:T(8,128)}, u32[]{:S(2)}) copy-start(f32[12,64]{1,0:T(8,128)} %get-tuple-element.116) | copy-start | bytes 9220
  464.6 162.3 %copy-start.10 = (bf16[3,128,12,64]{1,0,3,2:T(4,128)(2,1)S(1)}, bf16[3,128,12,64]{1,0,3,2:T(4,128)(2,1)}, u32[]{:S(2)}) copy-start(bf16[3,128,12,64]{1,0,3,2:T(4,128)(2,1)} %copy-done.9) | copy-start | bytes 1769476
  628.9 45.5 %copy-start.8 = (bf16[3,128,12,64]{1,0,3,2:T(4,128)(2,1)S(1)}, bf16[3,128,12,64]{1,0,3,2:T(4,128)(2,1)}, u32[]{:S(2)}) copy-start(bf16[3,128,12,64]{1,0,3,2:T(4,128)(2,1)} %copy.72) | copy-start | bytes 1769476
  631.1 45.3 %copy-start.7 = (bf16[3,128,12,64]{1,0,3,2:T(4,128)(2,1)S(1)}, bf16[3,128,12,64]{1,0,3,2:T(4,128)(2,1)}, u32[]{:S(2)}) copy-start(bf16[3,128,12,64]{1,0,3,2:T(4,128)(2,1)} %copy.74) | copy-start | bytes 1769476
  (37 other events, 134.2 us)
Sparse Core Ops, SparseCore 0:
  14.1 53.3 all-gather.4
  69.6 48.7 all-gather.2
  183.4 46.2 reduce-scatter.26
  231.8 47.5 reduce-scatter.24
  282.6 41.9 reduce-scatter.18
  328.2 42.4 reduce-scatter.28
  374.1 42.4 reduce-scatter.32
  420.3 42.4 reduce-scatter.30
  466.3 76.4 reduce-scatter.20
  546.2 76.4 reduce-scatter.22
  626.7 83.2 all-reduce.13
where the time goes:
time: 737 us; the launch traced here: 727 us
  waiting for transfers between devices  440 us (60%)
  matrix products  95.6 us (13%)
  local copies, waits for them, and re-layouts  95.3 us (13%)
  blocking collectives  52.7 us (7%)
  other arithmetic  26.8 us (4%)
  between operations  16.1 us (2%)
    unnamed x16, waiting for transfers between devices  169 us
    reduce_scatter x1, waiting for transfers between devices, per_device(): lax.psum_scatter(g_w_inner, 'batch', scatter_dimension=0, tiled=True)  78.2 us
    reduce_scatter x1, waiting for transfers between devices, per_device(): lax.psum_scatter(g_w_outer, 'batch', scatter_dimension=0, tiled=True)  77.7 us
    unnamed x126, local copies, waits for them, and re-layouts  68.5 us
    all_gather x1, waiting for transfers between devices, per_device(): lax.all_gather(valued, 'blk', axis=1, tiled=True)  42.2 us
    psum x1, waiting for transfers between devices, per_device(): lax.psum(shares[0].astype(jnp.bfloat16), 'blk').astype(jnp.float32)  32 us
    unnamed x1, blocking collectives  25.1 us
    all_gather x1, waiting for transfers between devices, per_device(): lax.all_gather(keyed, 'blk', axis=1, tiled=True)  24.9 us
  transfers between devices with their start and end apart: 11, of which 10 were waited for; matrix products, arithmetic and copies ran while one was open for 18% of the time, Pallas kernels for 0%

commit v1 on v0

v1 whole, which is shorter than its diff:
```python
import functools
import math

import jax
import jax.numpy as jnp
from jax import lax
from jax.experimental import pallas as pl
from jax.experimental.pallas import tpu as pltpu
from jax.sharding import PartitionSpec as P

BF = jnp.bfloat16
F32 = jnp.float32
EPS = 1e-05
D = 768
PAIRS = 6
LANES = 128
BLOCK = 128
ROW = 512
FFT = 768
FFN = 4
EARLY = 9
CHUNKS = 12
MIB = 1 << 20


def dot(a, b):
    return jnp.dot(a, b, preferred_element_type=F32)


def dot_nt(a, b):
    return lax.dot_general(a, b, (((1,), (1,)), ((), ())), preferred_element_type=F32)


def dot_tn(a, b):
    return lax.dot_general(a, b, (((0,), (0,)), ((), ())), preferred_element_type=F32)


def place():
    z = lax.axis_index("blk")
    beta = lax.axis_index("batch")
    c = lax.rem(beta, 2)
    return z, beta, c, beta - c


def at(z, beta):
    return {"blk": z, "batch": beta}


def greet(devices):
    barrier = pltpu.get_barrier_semaphore()
    for device in devices:
        pl.semaphore_signal(barrier, inc=1, device_id=device, device_id_type=pl.DeviceIdType.MESH)
    pl.semaphore_wait(barrier, len(devices))


def column_mates(z, c, base):
    mates = [at(lax.rem(z + step, 4), base + core) for step in range(1, 4) for core in range(2)]
    return mates + [at(z, base + 1 - c)]


def remote(src, dst, send_sem, recv_sem, device):
    return pltpu.make_async_remote_copy(
        src_ref=src,
        dst_ref=dst,
        send_sem=send_sem,
        recv_sem=recv_sem,
        device_id=device,
        device_id_type=pl.DeviceIdType.MESH,
    )


class Mover:
    def __init__(self, z, c, base):
        self.z, self.c, self.base, self.sent = z, c, base, []

    def send(self, src, dst, send_sem, recv_sem, to_z, to_c, when=None):
        self_target = jnp.logical_and(to_z == self.z, to_c == self.c)
        other = jnp.logical_not(self_target)
        if when is not None:
            self_target = jnp.logical_and(self_target, when)
            other = jnp.logical_and(other, when)
        out = remote(src, dst, send_sem, recv_sem, at(to_z, self.base + to_c))

        @pl.when(self_target)
        def _():
            pltpu.make_async_copy(src, dst, recv_sem).start()

        @pl.when(other)
        def _():
            out.start()

        self.sent.append((other, out))

    def finish(self):
        for other, out in self.sent:

            @pl.when(other)
            def _(out=out):
                out.wait_send()

        self.sent = []


def landed(dst, sem):
    pltpu.make_async_copy(dst, dst, sem).wait()


def exchange_body(tok, seg, cot, x, segs, cotq, d_send, d_recv, f_send, g_send, g_recv, c_send, c_recv):
    z, beta, c, base = place()
    greet(column_mates(z, c, base))
    move = Mover(z, c, base)
    first, second = c == 0, c == 1
    routes = [(s, 0, s, first) for s in range(3)] + [
        (0, 0, 3, second),
        (1, 1, 0, second),
        (1, 1, 1, second),
        (2, 1, 2, second),
        (2, 1, 3, second),
    ]
    count = 0
    for slot, ab, chip, when in routes:
        for half in range(2):
            move.send(
                tok.at[slot, half], x.at[ab, z, half], d_send.at[count], d_recv.at[ab, z, half], chip, half, when
            )
            move.send(seg.at[slot], segs.at[ab, z], g_send.at[count], g_recv.at[ab, z], chip, half, when)
            count += 1
    deep, low = z // 2, lax.rem(z, 2)
    for slot in range(3):
        move.send(cot.at[slot], cotq.at[low], c_send.at[slot], c_recv.at[low], slot, deep, first)
    move.send(cot.at[0], cotq.at[low], c_send.at[3], c_recv.at[low], 3, deep, second)
    move.send(cot.at[1], cotq.at[2], c_send.at[4], c_recv.at[2], deep, low, second)
    move.send(cot.at[2], cotq.at[2], c_send.at[5], c_recv.at[2], 2 + deep, low, second)
    forwards = []
    for ab in range(2):
        for b in range(4):
            landed(x.at[ab, b, c], d_recv.at[ab, b, c])
            copy = remote(
                x.at[ab, b, c], x.at[ab, b, c], f_send.at[ab, b], d_recv.at[ab, b, c], at(z, base + 1 - c)
            )
            copy.start()
            forwards.append(copy)
    for ab in range(2):
        for b in range(4):
            landed(x.at[ab, b, 1 - c], d_recv.at[ab, b, 1 - c])
            landed(segs.at[ab, b], g_recv.at[ab, b])
    for slot in range(3):
        landed(cotq.at[slot], c_recv.at[slot])
    for copy in forwards:
        copy.wait_send()
    move.finish()


def exchange(tokens, segments, cotangent):
    vmem = pl.BlockSpec(memory_space=pltpu.VMEM)
    dma = pltpu.SemaphoreType.DMA
    return pl.pallas_call(
        exchange_body,
        out_shape=(
            jax.ShapeDtypeStruct((2, 4, 2, 64, D), BF),
            jax.ShapeDtypeStruct((2, 4, 8, BLOCK), jnp.int32),
            jax.ShapeDtypeStruct((3, BLOCK, D), BF),
        ),
        in_specs=[vmem] * 3,
        out_specs=[vmem] * 3,
        scratch_shapes=[dma((16,)), dma((2, 4, 2)), dma((2, 4)), dma((16,)), dma((2, 4)), dma((6,)), dma((3,))],
        compiler_params=pltpu.CompilerParams(
            collective_id=0, has_side_effects=True, vmem_limit_bytes=16 * MIB
        ),
    )(tokens, segments, cotangent)


def lane_low():
    return lax.broadcasted_iota(jnp.int32, (BLOCK, LANES), 1) < 64


def stack_heads(pair, low):
    zero = jnp.zeros_like(pair)
    return jnp.concatenate([jnp.where(low, pair, zero), jnp.where(low, zero, pair)], axis=0)


def merge_heads(both, low):
    return jnp.where(low, both[:BLOCK], both[BLOCK:])


def moments(resid):
    center = resid - jnp.mean(resid, axis=-1, keepdims=True)
    inverse = lax.rsqrt(jnp.mean(center * center, axis=-1, keepdims=True) + EPS)
    return center * inverse, inverse


def norm_back(upstream, unit, inverse, gain):
    scaled = upstream * gain
    return inverse * (
        scaled
        - jnp.mean(scaled, axis=-1, keepdims=True)
        - unit * jnp.mean(scaled * unit, axis=-1, keepdims=True)
    )


def column_sum(value):
    return jnp.sum(value, axis=0, keepdims=True)


def forward_body(
    x,
    segs,
    cot,
    w_query,
    b_query,
    w_key,
    w_value,
    b_value,
    w_out,
    b_out,
    gain_first,
    shift_first,
    w_inner,
    b_inner,
    w_outer,
    b_outer,
    gain_second,
    shift_second,
    q,
    k,
    v,
    prob,
    att,
    d_att,
    d_first,
    xq,
    layer,
    early,
    vec,
    bias,
    unit1,
    inv1,
    low1,
    act,
    slope,
    acc,
    d_out,
):
    z, beta, c, base = place()
    low = lane_low()
    tokens = 3 * BLOCK
    vec[...] = jnp.zeros_like(vec)
    own = [(0, 2 * c), (0, 2 * c + 1), (1, 2 * lax.rem(z, 2) + c)]
    for u, (ab, b) in enumerate(own):
        xq[u] = x[ab, b].reshape(BLOCK, D)

    def one_hot(row):
        return (lax.broadcasted_iota(jnp.int32, (8, BLOCK), 0) == row).astype(F32)

    for u, (ab, b) in enumerate(own):
        mine = one_hot(segs[ab, b])
        for kb in range(4):
            same = dot_tn(mine, one_hot(segs[ab, kb]))
            bias[u, :, kb * BLOCK : (kb + 1) * BLOCK] = jnp.where(same > 0.5, 0.0, -1e30)

    xq_all = xq[...].reshape(tokens, D)
    q[...] = ((dot(xq_all, w_query[...]) + b_query[...]).astype(BF) * 0.125).astype(BF).reshape(3, BLOCK, D)
    for ab in range(2):
        xk = x[ab].reshape(ROW, D)
        k[ab] = dot(xk, w_key[...]).astype(BF)
        v[ab] = (dot(xk, w_value[...]) + b_value[...]).astype(BF)

    def attend(n, carry):
        u, j = n // PAIRS, lax.rem(n, PAIRS)
        ab = u // 2
        cols = pl.ds(pl.multiple_of(j * LANES, LANES), LANES)
        score = dot_nt(stack_heads(q[u, :, cols], low), k[ab, :, cols])
        score = (score.reshape(2, BLOCK, ROW) + bias[u][None]).reshape(2 * BLOCK, ROW)
        expo = jnp.exp(score - jnp.max(score, axis=-1, keepdims=True))
        p = (expo * (1.0 / jnp.sum(expo, axis=-1, keepdims=True))).astype(BF)
        prob[n] = p
        att[u, :, cols] = merge_heads(dot(p, v[ab, :, cols]), low).astype(BF)
        return carry

    lax.fori_loop(0, 3 * PAIRS, attend, 0)

    acc[...] = dot(att[...].reshape(tokens, D), w_out[...]).reshape(3, BLOCK, D)

    def norm_one(u, carry):
        first = xq[u].astype(F32) + acc[u] + b_out[...]
        unit, inverse = moments(first)
        unit1[u] = unit
        inv1[u] = jnp.broadcast_to(inverse, (BLOCK, LANES))
        low1[u] = (unit * gain_first[...] + shift_first[...]).astype(BF)
        return carry

    lax.fori_loop(0, 3, norm_one, 0)
    acc[...] = jnp.zeros_like(acc)

    def feed(f, carry):
        cols = pl.ds(pl.multiple_of(f * FFT, FFT), FFT)
        pre = dot(low1[...].reshape(tokens, D), w_inner[:, cols]) + b_inner[:, cols]
        half = 0.5 * (1.0 + lax.erf(pre * (1.0 / math.sqrt(2.0))))
        slope[f] = (half + pre * jnp.exp(-0.5 * pre * pre) * (1.0 / math.sqrt(2.0 * math.pi))).astype(BF)
        act_low = (pre * half).astype(BF)
        act[f] = act_low
        acc[...] += dot(act_low, w_outer[cols, :]).reshape(3, BLOCK, D)
        return carry

    lax.fori_loop(0, FFN, feed, 0)

    def norm_two(u, carry):
        second = unit1[u] * gain_first[...] + shift_first[...] + acc[u] + b_outer[...]
        unit, inverse = moments(second)
        layer[u] = (unit * gain_second[...] + shift_second[...]).astype(BF)
        up = cot[u].astype(F32)
        d_second = norm_back(up, unit, inverse, gain_second[...])
        d_low = d_second.astype(BF)
        acc[u] = d_second
        d_out[u] = d_low
        vec[5:6] += column_sum(d_low.astype(F32))
        vec[6:7] += column_sum(up * unit)
        vec[7:8] += column_sum(up)
        return carry

    lax.fori_loop(0, 3, norm_two, 0)

    def feed_back(f, carry):
        cols = pl.ds(pl.multiple_of(f * FFT, FFT), FFT)
        up = d_out[...].reshape(tokens, D)
        d_pre = (dot_nt(up, w_outer[cols, :]) * slope[f].astype(F32)).astype(BF)
        vec[pl.ds(8 + f, 1)] = column_sum(d_pre.astype(F32))
        g_outer = dot_tn(act[f], up).astype(BF)
        for piece in range(2):
            for part in range(4):
                row = 384 * piece + 96 * part
                early[part, piece, f] = g_outer[row : row + 96].reshape(2, 48, D)
        g_inner = dot_tn(low1[...].reshape(tokens, D), d_pre).astype(BF)
        for p in range(8):
            early[4 + f, p % 2, p // 2] = g_inner[96 * p : 96 * p + 96].reshape(2, 48, D)
        acc[...] += dot_nt(d_pre, w_inner[:, cols]).reshape(3, BLOCK, D)
        return carry

    lax.fori_loop(0, FFN, feed_back, 0)

    def norm_one_back(u, carry):
        up = acc[u]
        inner = norm_back(up, unit1[u], inv1[u][:, 0:1], gain_first[...])
        d_first[u] = inner
        d_low = inner.astype(BF)
        d_out[u] = d_low
        vec[2:3] += column_sum(d_low.astype(F32))
        vec[3:4] += column_sum(up * unit1[u])
        vec[4:5] += column_sum(up)
        return carry

    lax.fori_loop(0, 3, norm_one_back, 0)
    up = d_out[...].reshape(tokens, D)
    d_att[...] = dot_nt(up, w_out[...]).astype(BF).reshape(3, BLOCK, D)
    g_out = dot_tn(att[...].reshape(tokens, D), up).astype(BF)
    for p in range(8):
        early[8, p % 2, p // 2] = g_out[96 * p : 96 * p + 96].reshape(2, 48, D)


def forward(x, segs, cot, weights):
    vmem = pl.BlockSpec(memory_space=pltpu.VMEM)
    tok = (3, BLOCK, D)
    shapes = [
        (tok, BF),
        ((2, ROW, D), BF),
        ((2, ROW, D), BF),
        ((3 * PAIRS, 2 * BLOCK, ROW), BF),
        (tok, BF),
        (tok, BF),
        (tok, F32),
        (tok, BF),
        (tok, BF),
        ((EARLY, 2, 4, 2, 48, D), BF),
        ((16, D), F32),
    ]
    args = (x, segs, cot) + weights
    return pl.pallas_call(
        forward_body,
        out_shape=tuple(jax.ShapeDtypeStruct(s, t) for s, t in shapes),
        in_specs=[vmem] * len(args),
        out_specs=[vmem] * len(shapes),
        scratch_shapes=[
            pltpu.VMEM((3, BLOCK, ROW), F32),
            pltpu.VMEM(tok, F32),
            pltpu.VMEM((3, BLOCK, LANES), F32),
            pltpu.VMEM(tok, BF),
            pltpu.VMEM((FFN, 3 * BLOCK, FFT), BF),
            pltpu.VMEM((FFN, 3 * BLOCK, FFT), BF),
            pltpu.VMEM(tok, F32),
            pltpu.VMEM(tok, BF),
        ],
        compiler_params=pltpu.CompilerParams(vmem_limit_bytes=62 * MIB),
    )(*args)


def backward_body(
    x,
    xq,
    q,
    k,
    v,
    prob,
    att,
    d_att,
    d_first,
    layer,
    early,
    vec_in,
    w_query,
    w_key,
    w_value,
    sums,
    vec_out,
    lay_out,
    grad_parts,
    own,
    late,
    r1,
    r2,
    r3,
    ro,
    rj,
    dq,
    dkt,
    dvt,
    dk,
    dv,
    dx,
    dxs,
    rxa,
    rxb,
    sv,
    rv,
    own_sem,
    s1,
    t1,
    s2,
    t2,
    s3,
    t3,
    so,
    to,
    sj,
    tj,
    sf,
    tf,
    lay_s,
    lay_r,
    xs,
    xr,
    gs,
    gr,
    vs,
    vr,
):
    z, beta, c, base = place()
    low = lane_low()
    bx, by = lax.rem(beta // 2, 2), lax.rem(beta // 4, 2)
    sibling = at(z, base + 1 - c)
    to_x, to_y = at(z, beta + 2 - 4 * bx), at(z, beta + 4 - 8 * by)
    greet(column_mates(z, c, base) + [to_x, to_y])
    inner = jnp.logical_and(z > 0, z < 3)
    outer = jnp.logical_not(inner)
    half = lax.rem(z + 1, 2)
    mine = jnp.where(z == 2, 1, 0)
    neighbour = jnp.where(z < 2, 1 - z, 5 - z)
    partner = jnp.where(z == 1, 2, 1)
    near, across = at(neighbour, beta), at(partner, beta)
    tokens = 3 * BLOCK

    def fetch_own(i):
        return pltpu.make_async_copy(early.at[i, c], own.at[i], own_sem.at[i])

    def first_send(i, src):
        return remote(src, r1.at[i], s1.at[i], t1.at[i], sibling)

    for i in range(EARLY):
        first_send(i, early.at[i, 1 - c]).start()
        fetch_own(i).start()

    move = Mover(z, c, base)
    row_core = jnp.where(z == 3, 1, 0)
    row_slot = lax.rem(z, 3)
    deep, lowz = z // 2, lax.rem(z, 2)
    move.send(layer.at[0], lay_out.at[row_slot], lay_s.at[0], lay_r.at[row_slot], 2 * c, row_core)
    move.send(layer.at[1], lay_out.at[row_slot], lay_s.at[1], lay_r.at[row_slot], 2 * c + 1, row_core)
    move.send(layer.at[2], lay_out.at[1 + deep], lay_s.at[2], lay_r.at[1 + deep], 2 * lowz + c, 1)

    def split(i):
        t = lax.rem(i, 2)
        return t, 1 - t

    def sent_piece(i, e):
        t, s = split(i)
        return t * (2 * (1 - by) + e) + s * (2 * e + 1 - bx)

    def kept_piece(i, e):
        t, s = split(i)
        return t * (2 * by + e) + s * (2 * e + bx)

    def second_to(i):
        t, s = split(i)
        return at(z, beta + s * (2 - 4 * bx) + t * (4 - 8 * by))

    def third_to(i):
        t, s = split(i)
        return at(z, beta + t * (2 - 4 * bx) + s * (4 - 8 * by))

    def kept_half(i):
        t, s = split(i)
        return t * bx + s * by

    def second_send(i, e):
        return remote(r1.at[i, sent_piece(i, e)], r2.at[i, e], s2.at[i, e], t2.at[i, e], second_to(i))

    def third_send(i):
        return remote(r2.at[i, 1 - kept_half(i)], r3.at[i], s3.at[i], t3.at[i], third_to(i))

    def outer_send(i):
        return remote(r3.at[i], ro.at[i], so.at[i], to.at[i], near)

    def cross_send(i):
        return remote(r3.at[i, 1 - mine], rj.at[i], sj.at[i], tj.at[i], across)

    def final_near(i):
        return remote(sums.at[i, mine], sums.at[i, mine], sf.at[i, 0], tf.at[i, mine], near)

    def final_across(i):
        return remote(sums.at[i, mine], sums.at[i, mine], sf.at[i, 1], tf.at[i, mine], across)

    def final_forward(i):
        return remote(sums.at[i, 1 - mine], sums.at[i, 1 - mine], sf.at[i, 2], tf.at[i, 1 - mine], near)

    def wide(value):
        return value.astype(F32)

    def stage2(i):
        @pl.when(i < EARLY)
        def _():
            fetch_own(i).wait()

        landed(r1.at[i], t1.at[i])
        for e in range(2):
            p = sent_piece(i, e)
            r1[i, p] = (wide(r1[i, p]) + wide(own[i, p])).astype(BF)
            second_send(i, e).start()

    def stage3(i):
        for e in range(2):
            landed(r2.at[i, e], t2.at[i, e])
        e = 1 - kept_half(i)
        p = kept_piece(i, e)
        r2[i, e] = (wide(r2[i, e]) + wide(r1[i, p]) + wide(own[i, p])).astype(BF)
        third_send(i).start()

    def stage4(i):
        landed(r3.at[i], t3.at[i])
        e = kept_half(i)
        p = kept_piece(i, e)
        total = wide(r2[i, e]) + wide(r1[i, p]) + wide(own[i, p]) + wide(r3[i])
        r3[i] = total.astype(BF)

        @pl.when(outer)
        def _():
            outer_send(i).start()

    def stage5(i):
        @pl.when(inner)
        def _():
            landed(ro.at[i], to.at[i])
            r3[i, 1 - mine] = (wide(r3[i, 1 - mine]) + wide(ro[i, 1 - mine])).astype(BF)
            cross_send(i).start()

    def stage6(i):
        @pl.when(inner)
        def _():
            landed(rj.at[i], tj.at[i])
            sums[i, mine] = (wide(r3[i, mine]) + wide(ro[i, mine]) + wide(rj[i])).astype(BF)
            final_near(i).start()
            final_across(i).start()

    def stage7(i):
        @pl.when(inner)
        def _():
            landed(sums.at[i, 1 - mine], tf.at[i, 1 - mine])
            final_forward(i).start()

    stages = [stage2, stage3, stage4, stage5, stage6, stage7]

    def tick(n):
        for lag, stage in enumerate(stages):
            i = n - lag

            @pl.when(jnp.logical_and(i >= 0, i < CHUNKS))
            def _(i=i, stage=stage):
                stage(i)

    def attend_back(n):
        u, j = n // PAIRS, lax.rem(n, PAIRS)
        ab = u // 2
        cols = pl.ds(pl.multiple_of(j * LANES, LANES), LANES)
        d_pair = d_att[u, :, cols]
        d_both = stack_heads(d_pair, low)
        product = wide(d_pair) * wide(att[u, :, cols])
        even = jnp.sum(jnp.where(low, product, 0.0), axis=-1, keepdims=True)
        odd = jnp.sum(jnp.where(low, 0.0, product), axis=-1, keepdims=True)
        centre = jnp.concatenate([even, odd], axis=0)
        p = prob[n]
        d_prob = dot_nt(d_both, v[ab, :, cols])
        d_score = (wide(p) * (d_prob - centre)).astype(BF)
        dq[u, :, cols] = (merge_heads(dot(d_score, k[ab, :, cols]), low) * 0.125).astype(BF)
        q_both = stack_heads(q[u, :, cols], low)
        g_key = dot(q_both.T, d_score)
        g_value = dot(d_both.T, p)

        @pl.when(u == 1)
        def _():
            dkt[ab, cols, :] += g_key
            dvt[ab, cols, :] += g_value

        @pl.when(u != 1)
        def _():
            dkt[ab, cols, :] = g_key
            dvt[ab, cols, :] = g_value

    def step(n, carry):
        attend_back(n)

        @pl.when(lax.rem(n, 3) == 2)
        def _():
            tick(n // 3)

        return carry

    lax.fori_loop(0, 3 * PAIRS, step, 0)
    done = PAIRS

    for ab in range(2):
        dk[ab] = dkt[ab].astype(BF).T
        dv[ab] = dvt[ab].astype(BF).T

    def keep_late(i, grad):
        low_grad = grad.astype(BF)
        for p in range(8):
            late[i, p % 2, p // 2] = low_grad[96 * p : 96 * p + 96].reshape(2, 48, D)
        first_send(EARLY + i, late.at[i, 1 - c]).start()
        own[EARLY + i] = late[i, c]

    keep_late(0, dot_tn(xq[...].reshape(tokens, D), dq[...].reshape(tokens, D)))
    tick(done)
    keep_late(1, dot_tn(x[...].reshape(2 * ROW, D), dk[...].reshape(2 * ROW, D)))
    keep_late(2, dot_tn(x[...].reshape(2 * ROW, D), dv[...].reshape(2 * ROW, D)))
    tick(done + 1)
    sv[0] = vec_in[...]
    sv[0, 0:1] = column_sum(wide(dq[...].reshape(tokens, D)))
    sv[0, 1:2] = column_sum(wide(dv[...].reshape(2 * ROW, D)))

    vec_to = [sibling, to_x, to_y, at(z + 1 - 2 * lowz, beta), at(z + 2 - 4 * deep, beta)]

    def vec_send(i):
        return remote(sv.at[i], rv.at[i], vs.at[i], vr.at[i], vec_to[i])

    vec_send(0).start()

    for ab in range(2):
        part = dot_nt(dk[ab], w_key[...]) + dot_nt(dv[ab], w_value[...])
        dx[ab] = part.reshape(4, BLOCK, D)
    query_part = dot_nt(dq[...].reshape(tokens, D), w_query[...]).reshape(3, BLOCK, D)
    blocks = [(0, 2 * c), (0, 2 * c + 1), (1, 2 * lowz + c)]
    for u, (ab, b) in enumerate(blocks):
        dx[ab, b] += query_part[u] + d_first[u]
    dxs[...] = dx[...].astype(BF)
    swap = [
        remote(dxs.at[0, 2 * (1 - c) + e], rxa.at[e], xs.at[0, e], xr.at[0, e], sibling) for e in range(2)
    ] + [remote(dxs.at[1, 1 - c + 2 * e], rxb.at[e], xs.at[1, e], xr.at[1, e], sibling) for e in range(2)]
    for copy in swap:
        copy.start()
    tick(done + 2)
    for e in range(2):
        landed(rxa.at[e], xr.at[0, e])
        rxa[e] = (dx[0, 2 * c + e] + wide(rxa[e])).astype(BF)
        move.send(rxa.at[e], grad_parts.at[row_slot, 0], gs.at[e], gr.at[row_slot, 0], 2 * c + e, row_core)
    for e in range(2):
        landed(rxb.at[e], xr.at[1, e])
        rxb[e] = (dx[1, c + 2 * e] + wide(rxb[e])).astype(BF)
        move.send(rxb.at[e], grad_parts.at[1 + deep, lowz], gs.at[2 + e], gr.at[1 + deep, lowz], c + 2 * e, 1)
    done += 3

    def vec_stage(i):
        landed(rv.at[i], vr.at[i])
        total = sv[i] + rv[i]
        if i < 4:
            sv[i + 1] = total
            vec_send(i + 1).start()
        else:
            vec_out[...] = total

    for i in range(5):
        tick(done + i)
        vec_stage(i)
    done += 5

    def rest(n, carry):
        tick(n)
        return carry

    lax.fori_loop(done, CHUNKS + len(stages) - 1, rest, 0)

    def close(i, carry):
        first_send(i, own.at[i]).wait_send()
        for e in range(2):
            second_send(i, e).wait_send()
        third_send(i).wait_send()

        @pl.when(outer)
        def _():
            outer_send(i).wait_send()
            landed(sums.at[i, 0], tf.at[i, 0])
            landed(sums.at[i, 1], tf.at[i, 1])

        @pl.when(inner)
        def _():
            cross_send(i).wait_send()
            final_near(i).wait_send()
            final_across(i).wait_send()
            final_forward(i).wait_send()

        return carry

    lax.fori_loop(0, CHUNKS, close, 0)
    for i in range(5):
        vec_send(i).wait_send()
    for copy in swap:
        copy.wait_send()
    for slot in range(3):
        landed(lay_out.at[slot], lay_r.at[slot])
        landed(grad_parts.at[slot, 0], gr.at[slot, 0])

    @pl.when(c == 1)
    def _():
        for slot in range(1, 3):
            landed(grad_parts.at[slot, 1], gr.at[slot, 1])

    move.finish()


def backward(x, xq, q, k, v, prob, att, d_att, d_first, layer, early, vec, w_query, w_key, w_value):
    vmem = pl.BlockSpec(memory_space=pltpu.VMEM)
    dma = pltpu.SemaphoreType.DMA
    args = (x, xq, q, k, v, prob, att, d_att, d_first, layer, early, vec, w_query, w_key, w_value)
    specs = [vmem] * len(args)
    specs[10] = pl.BlockSpec(memory_space=pl.ANY)
    n = CHUNKS
    return pl.pallas_call(
        backward_body,
        out_shape=(
            jax.ShapeDtypeStruct((n, 2, 48, D), BF),
            jax.ShapeDtypeStruct((16, D), F32),
            jax.ShapeDtypeStruct((3, BLOCK, D), BF),
            jax.ShapeDtypeStruct((3, 2, BLOCK, D), BF),
        ),
        in_specs=specs,
        out_specs=[vmem] * 4,
        scratch_shapes=[
            pltpu.VMEM((n, 4, 2, 48, D), BF),
            pltpu.VMEM((3, 2, 4, 2, 48, D), BF),
            pltpu.VMEM((n, 4, 2, 48, D), BF),
            pltpu.VMEM((n, 2, 2, 48, D), BF),
            pltpu.VMEM((n, 2, 48, D), BF),
            pltpu.VMEM((n, 2, 48, D), BF),
            pltpu.VMEM((n, 48, D), BF),
            pltpu.VMEM((3, BLOCK, D), BF),
            pltpu.VMEM((2, D, ROW), F32),
            pltpu.VMEM((2, D, ROW), F32),
            pltpu.VMEM((2, ROW, D), BF),
            pltpu.VMEM((2, ROW, D), BF),
            pltpu.VMEM((2, 4, BLOCK, D), F32),
            pltpu.VMEM((2, 4, BLOCK, D), BF),
            pltpu.VMEM((2, BLOCK, D), BF),
            pltpu.VMEM((2, BLOCK, D), BF),
            pltpu.VMEM((5, 16, D), F32),
            pltpu.VMEM((5, 16, D), F32),
            dma((n,)),
            dma((n,)),
            dma((n,)),
            dma((n, 2)),
            dma((n, 2)),
            dma((n,)),
            dma((n,)),
            dma((n,)),
            dma((n,)),
            dma((n,)),
            dma((n,)),
            dma((n, 3)),
            dma((n, 2)),
            dma((3,)),
            dma((3,)),
            dma((2, 2)),
            dma((2, 2)),
            dma((4,)),
            dma((3, 2)),
            dma((5,)),
            dma((5,)),
        ],
        compiler_params=pltpu.CompilerParams(
            collective_id=1, has_side_effects=True, vmem_limit_bytes=63 * MIB
        ),
    )(*args)


def finish_body(sums, vec, lay, parts, *outs):
    p = lax.rem(lax.axis_index("batch"), 8)
    c = lax.rem(p, 2)
    layer_out, input_grad, g_q, g_k, g_v, g_o, g_inner, g_outer, vecs, b_inner = outs
    layer_out[...] = lay[...]
    input_grad[...] = parts[:, 0]

    @pl.when(c == 1)
    def _():
        for slot in range(1, 3):
            input_grad[slot] = (parts[slot, 0].astype(F32) + parts[slot, 1].astype(F32)).astype(BF)

    def piece(i):
        return sums[i].reshape(96, D).astype(F32)

    for part in range(4):
        g_outer[96 * part : 96 * part + 96] = piece(part)
    for f in range(FFN):
        g_inner[:, f * FFT : (f + 1) * FFT] = piece(4 + f)
    g_o[...] = piece(8)
    g_q[...] = piece(9)
    g_k[...] = piece(10)
    g_v[...] = piece(11)
    pick = lax.broadcasted_iota(jnp.int32, (D, LANES), 0) == lax.broadcasted_iota(jnp.int32, (D, LANES), 1) + 96 * p
    vecs[...] = jnp.dot(
        vec[0:8], pick.astype(F32), preferred_element_type=F32, precision=lax.Precision.HIGHEST
    )
    b_inner[...] = vec[pl.ds(8 + p // 2, 1), pl.ds(pl.multiple_of(384 * lax.rem(p, 2), LANES), 384)]


def finish(sums, vec, lay, parts):
    vmem = pl.BlockSpec(memory_space=pltpu.VMEM)
    tok = (3, BLOCK, D)
    shapes = [
        (tok, BF),
        (tok, BF),
        ((96, D), F32),
        ((96, D), F32),
        ((96, D), F32),
        ((96, D), F32),
        ((96, 4 * D), F32),
        ((384, D), F32),
        ((8, LANES), F32),
        ((1, 384), F32),
    ]
    return pl.pallas_call(
        finish_body,
        out_shape=tuple(jax.ShapeDtypeStruct(s, t) for s, t in shapes),
        in_specs=[vmem] * 4,
        out_specs=[vmem] * len(shapes),
        compiler_params=pltpu.CompilerParams(vmem_limit_bytes=32 * MIB),
    )(sums, vec, lay, parts)


def per_device(
    groups,
    tokens,
    segment_ids,
    w_query,
    b_query,
    w_key,
    w_value,
    b_value,
    w_out,
    b_out,
    gain_first,
    shift_first,
    w_inner,
    b_inner,
    w_outer,
    b_outer,
    gain_second,
    shift_second,
    cotangent,
):
    def row(value):
        return value.reshape(1, -1)

    seg = jnp.broadcast_to(segment_ids[:, None, :], (3, 8, BLOCK))
    x, segs, cot = exchange(tokens.reshape(3, 2, 64, D), seg, cotangent)
    weights = (
        w_query,
        row(b_query),
        w_key,
        w_value,
        row(b_value),
        w_out,
        row(b_out),
        row(gain_first),
        row(shift_first),
        w_inner,
        row(b_inner),
        w_outer,
        row(b_outer),
        row(gain_second),
        row(shift_second),
    )
    q, k, v, prob, att, d_att, d_first, xq, layer, early, vec = forward(x, segs, cot, weights)
    sums, vec, lay, parts = backward(
        x, xq, q, k, v, prob, att, d_att, d_first, layer, early, vec, w_query, w_key, w_value
    )
    layer_out, input_grad, g_q, g_k, g_v, g_o, g_inner, g_outer, vecs, g_b_inner = finish(sums, vec, lay, parts)
    vecs = [vecs[i, :96] for i in range(8)]
    g_b_query, g_b_value, g_b_out, g_gain_first, g_shift_first, g_b_outer, g_gain_second, g_shift_second = vecs
    grads = (
        g_q,
        g_b_query,
        g_k,
        g_v,
        g_b_value,
        g_o,
        g_b_out,
        g_gain_first,
        g_shift_first,
        g_inner,
        g_b_inner.reshape(384),
        g_outer,
        g_b_outer,
        g_gain_second,
        g_shift_second,
    )
    if groups > 1:
        place_at = lax.rem(lax.axis_index("batch"), 8)

        def spread(grad):
            whole = jnp.zeros((8 * grad.shape[0],) + grad.shape[1:], grad.dtype)
            whole = lax.dynamic_update_slice_in_dim(whole, grad, place_at * grad.shape[0], 0)
            return lax.psum_scatter(whole, "batch", scatter_dimension=0, tiled=True)

        grads = tuple(spread(grad) for grad in grads)
    return (layer_out, input_grad) + grads


def solution(mesh):
    tokens = P("batch", "blk", None)
    weight, vector = P("batch", None), P("batch")
    return jax.shard_map(
        functools.partial(per_device, mesh.shape["batch"] // 8),
        mesh=mesh,
        in_specs=(tokens, P("batch", "blk")) + (P(),) * 15 + (tokens,),
        out_specs=(tokens, tokens)
        + (
            weight,
            vector,
            weight,
            weight,
            vector,
            weight,
            vector,
            vector,
            vector,
            weight,
            vector,
            weight,
            vector,
            vector,
            vector,
        ),
        check_vma=False,
    )
```

time: 737 us -> 226 us (0.31); the launches traced: 727 us -> 225 us
  waiting for transfers between devices: 440 us -> 0 us
  Pallas kernels: 0 us -> 203 us
  matrix products: 95.6 us -> 0 us
  local copies, waits for them, and re-layouts: 95.3 us -> 20.7 us
  blocking collectives: 52.7 us -> 0 us
  other arithmetic: 26.8 us -> 0.6 us
  between operations: 16.1 us -> 0.7 us
    pallas_call x0 -> x4, Pallas kernels: none -> 203 us  [the longest x1 127 us: backward(): pl.pallas_call(backward_body, out_shape=(jax.ShapeDtypeStruct((n, 2, 48,...]
    reduce_scatter x3 -> x0, waiting for transfers between devices: 172 us -> none  [the longest x1 78.2 us: per_device(): lax.psum_scatter(g_w_inner, 'batch', scatter_dimension=0, tiled=True)]
    unnamed x16 -> x0, waiting for transfers between devices: 169 us -> none
    dot_general x23 -> x0, matrix products: 86.9 us -> none  [the longest x6 21.2 us: matmul(): return jnp.dot(left, right, preferred_element_type=jnp.float32)]
    all_gather x2 -> x0, waiting for transfers between devices: 67.2 us -> none  [the longest x1 42.2 us: per_device(): lax.all_gather(valued, 'blk', axis=1, tiled=True)]
    unnamed x126 -> x18, local copies, waits for them, and re-layouts: 68.5 us -> 9.34 us
    psum x1 -> x0, waiting for transfers between devices: 32 us -> none  [per_device(): lax.psum(shares[0].astype(jnp.bfloat16), 'blk').astype(jnp.float32)]
    unnamed x1 -> x0, blocking collectives: 25.1 us -> none
  transfers between devices with their start and end apart: 11 -> 0, of which waited for: 10 -> 0; matrix products, arithmetic and copies ran while one was open for 18% -> 0% of each run, Pallas kernels for 0% -> 0%
where the time goes in v1:
time: 226 us; the launch traced here: 225 us
  Pallas kernels  203 us (90%)
  local copies, waits for them, and re-layouts  20.7 us (9%)
    pallas_call x1, Pallas kernels, backward(): pl.pallas_call(backward_body, out_shape=(jax.ShapeDtypeStruct((n, 2, 48,...  127 us
    pallas_call x1, Pallas kernels, forward(): pl.pallas_call(forward_body, out_shape=tuple((jax.ShapeDtypeStruct(s, t)...  46.3 us
    pallas_call x1, Pallas kernels, exchange(): pl.pallas_call(exchange_body, out_shape=(jax.ShapeDtypeStruct((2, 4, 2, 6...  26.8 us
    reshape x8, local copies, waits for them, and re-layouts, row(): return value.reshape(1, -1)  10.2 us
    unnamed x18, local copies, waits for them, and re-layouts  9.34 us

profile of v1, /device:TPU:0, one launch (start us, length us, event | category | flops | bytes accessed | tf_op | source)
XLA Modules:
  0.0 224.7 jit_solution(3242342516820807153)
XLA Ops:
  0.7 1.3 reshape.69.b_query
  1.9 1.3 reshape.70.b_value
  3.2 1.3 reshape.71.b_out
  4.5 1.3 reshape.72.gain_first
  5.7 1.3 reshape.73.shift_first
  7.0 1.3 reshape.75.b_outer
  8.3 1.3 reshape.76.gain_second
  9.6 1.3 reshape.77.shift_second
  10.8 0.7 broadcast_in_dim.2.seg
  11.5 1.1 copy-done.5
  12.6 1.1 copy-done.6
  13.6 26.8 %shard_map.305 = (bf16[2,4,2,64,768]{4,3,2,1,0:T(8,128)(2,1)S(1)}, s32[2,4,8,128]{3,2,1,0:T(8,128)S(1)}, bf16[3,128,768]{2,1,0:T(8,128)(2,1)S(1)}) custom-call(bf16[3,2,64,768]{3,2,1,0:T(8,128)(2,1)S(1)} %bitcast.18, s32[3,8,128]{2,1,0:T(8,128)S(1)} %broadcast_in_dim.2.seg, bf16[3,128,768]{2,1,0:T(8,128)(2,1)S(1)} %copy-done.6), custom_call_target="tpu_custom_call" | custom-call | tf_op jit(solution)/shard_map/pallas_call | solution.py:157
  40.5 1.2 copy-done
  41.7 0.8 copy-done.3
  42.5 0.6 copy-done.8
  43.1 46.3 %shard_map.306 = (bf16[3,128,768]{2,1,0:T(8,128)(2,1)}, bf16[2,512,768]{2,1,0:T(8,128)(2,1)}, bf16[2,512,768]{2,1,0:T(8,128)(2,1)}, bf16[18,256,512]{2,1,0:T(8,1...) custom-call(bf16[2,4,2,64,768]{4,3,2,1,0:T(8,128)(2,1)} %copy-done, ...), custom_call_target="tpu_custom_call" | custom-call | tf_op jit(solution)/shard_map/pallas_call | solution.py:377
  89.4 127.3 %shard_map.307 = (bf16[12,2,48,768]{3,2,1,0:T(8,128)(2,1)}, f32[16,768]{1,0:T(8,128)}, bf16[3,128,768]{2,1,0:T(8,128)(2,1)}, bf16[3,2,128,768]{3,2,1,0:T(8,128)(2,1)}) custom-call(bf16[2,4,2,64,768]{4,3,2,1,0:T(8,128)(2,1)} %copy-done, bf16[3,128,768]{2,1,0:T(8,128)(2,1)} %get-tuple-element.48.xq, bf16[3,128,768]{2,1,0:T(8,128)(2,1)} %get-tuple-element.49.q, ...), custom_call_target="tpu_custom_call" | custom-call | tf_op jit(solution)/shard_map/pallas_call | solution.py:754
  216.7 1.5 copy-done.1
  218.2 1.3 copy-done.2
  219.4 1.1 copy-done.4
  220.5 0.8 copy-done.7
  221.3 2.3 %shard_map.308 = (bf16[3,128,768]{2,1,0:T(8,128)(2,1)}, bf16[3,128,768]{2,1,0:T(8,128)(2,1)}, f32[96,768]{1,0:T(8,128)}, f32[96,768]{1,0:T(8,128)}, f32[96,768]{...) custom-call(bf16[12,2,48,768]{3,2,1,0:T(8,128)(2,1)S(1)} %copy-done., ...), custom_call_target="tpu_custom_call" | custom-call | tf_op jit(solution)/shard_map/pallas_call | solution.py:856
  223.6 0.6 reduce
  224.2 0.5 slice_bitcast_fusion
  (9 shorter events, 0.0 us)
Async XLA Ops:
  11.5 1.1 copy-start.5
  12.6 1.1 copy-start.6
  40.5 1.2 copy-start
  41.7 0.8 copy-start.3
  42.5 0.6 copy-start.8
  216.7 1.5 copy-start.1
  218.2 1.3 copy-start.2
  219.4 1.1 copy-start.4
  220.5 0.8 copy-start.7

commit v2 on v1

v2 whole, which is shorter than its diff:
```python
import functools
import math

import jax
import jax.numpy as jnp
from jax import lax
from jax.experimental import pallas as pl
from jax.experimental.pallas import tpu as pltpu
from jax.sharding import PartitionSpec as P

BF = jnp.bfloat16
F32 = jnp.float32
EPS = 1e-05
D = 768
PAIRS = 6
LANES = 128
BLOCK = 128
ROW = 512
FFT = 768
FFN = 4
EARLY = 9
CHUNKS = 12
LAGS = (0, 2, 4, 5, 6, 7)
MIB = 1 << 20


def dot(a, b):
    return jnp.dot(a, b, preferred_element_type=F32)


def dot_nt(a, b):
    return lax.dot_general(a, b, (((1,), (1,)), ((), ())), preferred_element_type=F32)


def dot_tn(a, b):
    return lax.dot_general(a, b, (((0,), (0,)), ((), ())), preferred_element_type=F32)


def place():
    z = lax.axis_index("blk")
    beta = lax.axis_index("batch")
    c = lax.rem(beta, 2)
    return z, beta, c, beta - c


def at(z, beta):
    return {"blk": z, "batch": beta}


def greet(devices):
    barrier = pltpu.get_barrier_semaphore()
    for device in devices:
        pl.semaphore_signal(barrier, inc=1, device_id=device, device_id_type=pl.DeviceIdType.MESH)
    pl.semaphore_wait(barrier, len(devices))


def column_mates(z, c, base):
    mates = [at(lax.rem(z + step, 4), base + core) for step in range(1, 4) for core in range(2)]
    return mates + [at(z, base + 1 - c)]


def remote(src, dst, send_sem, recv_sem, device):
    return pltpu.make_async_remote_copy(
        src_ref=src,
        dst_ref=dst,
        send_sem=send_sem,
        recv_sem=recv_sem,
        device_id=device,
        device_id_type=pl.DeviceIdType.MESH,
    )


class Mover:
    def __init__(self, z, c, base):
        self.z, self.c, self.base, self.sent = z, c, base, []

    def send(self, src, dst, send_sem, recv_sem, to_z, to_c, when=None):
        self_target = jnp.logical_and(to_z == self.z, to_c == self.c)
        other = jnp.logical_not(self_target)
        if when is not None:
            self_target = jnp.logical_and(self_target, when)
            other = jnp.logical_and(other, when)
        out = remote(src, dst, send_sem, recv_sem, at(to_z, self.base + to_c))

        @pl.when(self_target)
        def _():
            pltpu.make_async_copy(src, dst, recv_sem).start()

        @pl.when(other)
        def _():
            out.start()

        self.sent.append((other, out))

    def finish(self):
        for other, out in self.sent:

            @pl.when(other)
            def _(out=out):
                out.wait_send()

        self.sent = []


def landed(dst, sem):
    pltpu.make_async_copy(dst, dst, sem).wait()


def lane_low():
    return lax.broadcasted_iota(jnp.int32, (BLOCK, LANES), 1) < 64


def stack_heads(pair, low):
    zero = jnp.zeros_like(pair)
    return jnp.concatenate([jnp.where(low, pair, zero), jnp.where(low, zero, pair)], axis=0)


def merge_heads(both, low):
    return jnp.where(low, both[:BLOCK], both[BLOCK:])


def moments(resid):
    center = resid - jnp.mean(resid, axis=-1, keepdims=True)
    inverse = lax.rsqrt(jnp.mean(center * center, axis=-1, keepdims=True) + EPS)
    return center * inverse, inverse


def norm_back(upstream, unit, inverse, gain):
    scaled = upstream * gain
    return inverse * (
        scaled
        - jnp.mean(scaled, axis=-1, keepdims=True)
        - unit * jnp.mean(scaled * unit, axis=-1, keepdims=True)
    )


def column_sum(value):
    return jnp.sum(value, axis=0, keepdims=True)


def layer_body(
    tok,
    seg,
    cot,
    w_query_in,
    w_key_in,
    w_value_in,
    w_out_in,
    w_inner_in,
    w_outer_in,
    b_query_in,
    b_value_in,
    b_out_in,
    gain_first_in,
    shift_first_in,
    b_outer_in,
    gain_second_in,
    shift_second_in,
    b_inner_in,
    sums,
    vec_out,
    lay_out,
    grad_parts,
    pool,
    w_outer,
    w_query,
    w_key,
    w_value,
    w_out,
    rows,
    b_inner,
    x,
    segs,
    cotq,
    q,
    k,
    v,
    att,
    low1,
    act,
    slope,
    acc,
    unit1,
    d_out,
    bias,
    lse,
    inv1,
    vec,
    r1,
    r2,
    r3,
    ro,
    rj,
    rxa,
    rxb,
    sv,
    rv,
    w_sem,
    d_send,
    d_recv,
    f_send,
    g_send,
    g_recv,
    c_send,
    c_recv,
    s1,
    t1,
    s2,
    t2,
    s3,
    t3,
    so,
    to,
    sj,
    tj,
    sf,
    tf,
    lay_s,
    lay_r,
    xs,
    xr,
    gs,
    gr,
    vs,
    vr,
):
    z, beta, c, base = place()
    low = lane_low()
    tokens = 3 * BLOCK
    bx, by = lax.rem(beta // 2, 2), lax.rem(beta // 4, 2)
    sibling = at(z, base + 1 - c)
    to_x, to_y = at(z, beta + 2 - 4 * bx), at(z, beta + 4 - 8 * by)
    inner = jnp.logical_and(z > 0, z < 3)
    outer = jnp.logical_not(inner)
    mine = jnp.where(z == 2, 1, 0)
    near = at(jnp.where(z < 2, 1 - z, 5 - z), beta)
    across = at(jnp.where(z == 1, 2, 1), beta)
    deep, lowz = z // 2, lax.rem(z, 2)

    loads = []

    def load(src, dst):
        copy = pltpu.make_async_copy(src, dst, w_sem.at[len(loads)])
        copy.start()
        loads.append(copy)
        return copy

    greet(column_mates(z, c, base) + [to_x, to_y])
    move = Mover(z, c, base)
    first, second = c == 0, c == 1
    routes = [(s, 0, s, first) for s in range(3)] + [
        (0, 0, 3, second),
        (1, 1, 0, second),
        (1, 1, 1, second),
        (2, 1, 2, second),
        (2, 1, 3, second),
    ]
    count = 0
    for slot, ab, chip, when in routes:
        for half in range(2):
            move.send(
                tok.at[slot, half], x.at[ab, z, half], d_send.at[count], d_recv.at[ab, z, half], chip, half, when
            )
            move.send(seg.at[slot], segs.at[ab, z, 0], g_send.at[count], g_recv.at[ab, z], chip, half, when)
            count += 1

    got_key = load(w_key_in, w_key)
    got_value = load(w_value_in, w_value)
    got_query = load(w_query_in, w_query)
    vectors = [b_query_in, b_value_in, b_out_in, gain_first_in, shift_first_in, b_outer_in, gain_second_in]
    got_rows = [load(ref, rows.at[i]) for i, ref in enumerate(vectors + [shift_second_in])]
    got_rows.append(load(b_inner_in, b_inner.at[0]))
    got_out = load(w_out_in, w_out)
    got_inner = [load(w_inner_in.at[:, :, f * FFT : (f + 1) * FFT], pool.at[EARLY + f]) for f in range(FFN)]
    got_outer = [load(w_outer_in.at[f], w_outer.at[f]) for f in range(FFN)]

    b_query, b_value, b_out, gain_first, shift_first, b_outer, gain_second, shift_second = (
        rows.at[i : i + 1] for i in range(8)
    )
    vec[...] = jnp.zeros_like(vec)
    forwards = []
    for ab in range(2):
        for b in range(4):
            landed(x.at[ab, b, c], d_recv.at[ab, b, c])
            copy = remote(x.at[ab, b, c], x.at[ab, b, c], f_send.at[ab, b], d_recv.at[ab, b, c], sibling)
            copy.start()
            forwards.append(copy)

    for slot in range(3):
        move.send(cot.at[slot], cotq.at[lowz], c_send.at[slot], c_recv.at[lowz], slot, deep, first)
    move.send(cot.at[0], cotq.at[lowz], c_send.at[3], c_recv.at[lowz], 3, deep, second)
    move.send(cot.at[1], cotq.at[2], c_send.at[4], c_recv.at[2], deep, lowz, second)
    move.send(cot.at[2], cotq.at[2], c_send.at[5], c_recv.at[2], 2 + deep, lowz, second)

    own_blocks = [(0, 2 * c), (0, 2 * c + 1), (1, 2 * lowz + c)]

    def own_tokens(u):
        ab, b = own_blocks[u]
        return x[ab, b].reshape(BLOCK, D)

    def one_hot(row):
        return (lax.broadcasted_iota(jnp.int32, (8, BLOCK), 0) == row).astype(F32)

    got_key.wait()
    got_value.wait()
    got_query.wait()
    for copy in got_rows:
        copy.wait()
    for ab in range(2):
        for b in range(4):
            landed(x.at[ab, b, 1 - c], d_recv.at[ab, b, 1 - c])
            landed(segs.at[ab, b, 0], g_recv.at[ab, b])
        xk = x[ab].reshape(ROW, D)
        k[ab] = dot(xk, w_key[...]).astype(BF)
        v[ab] = (dot(xk, w_value[...]) + b_value[...]).astype(BF)
        for u, (row, b) in enumerate(own_blocks):
            if row == ab:
                q[u] = ((dot(own_tokens(u), w_query[...]) + b_query[...]).astype(BF) * 0.125).astype(BF)
                own_hot = one_hot(segs[ab, b, 0:1])
                for kb in range(4):
                    same = dot_tn(own_hot, one_hot(segs[ab, kb, 0:1]))
                    bias[u, :, kb * BLOCK : (kb + 1) * BLOCK] = jnp.where(same > 0.5, 0.0, -1e30)

    def lanes(j):
        return pl.ds(pl.multiple_of(j * LANES, LANES), LANES)

    lane = lax.broadcasted_iota(jnp.int32, (BLOCK, LANES), 1)

    def scores(u, cols, keys):
        score = dot_nt(stack_heads(q[u, :, cols], low), keys)
        return (score.reshape(2, BLOCK, ROW) + bias[u][None]).reshape(2 * BLOCK, ROW)

    def attend(n, carry):
        u, j = n // PAIRS, lax.rem(n, PAIRS)
        ab, cols = u // 2, lanes(j)
        score = scores(u, cols, k[ab, :, cols])
        top = jnp.max(score, axis=-1, keepdims=True)
        expo = jnp.exp(score - top)
        total = jnp.sum(expo, axis=-1, keepdims=True)
        p = (expo * (1.0 / total)).astype(BF)
        stat = top + jnp.log(total)
        lse[u] = jnp.where(lane == 2 * j, stat[:BLOCK], jnp.where(lane == 2 * j + 1, stat[BLOCK:], lse[u]))
        att[u, :, cols] = merge_heads(dot(p, v[ab, :, cols]), low).astype(BF)
        return carry

    for copy in forwards:
        copy.wait_send()
    lse[...] = jnp.zeros_like(lse)
    lax.fori_loop(0, 3 * PAIRS, attend, 0)

    got_out.wait()
    acc[...] = dot(att[...].reshape(tokens, D), w_out[...]).reshape(3, BLOCK, D)
    for u in range(3):
        resid = own_tokens(u).astype(F32) + acc[u] + b_out[...]
        unit, inverse = moments(resid)
        unit1[u] = unit
        inv1[u] = jnp.broadcast_to(inverse, (BLOCK, LANES))
        low1[u] = (unit * gain_first[...] + shift_first[...]).astype(BF)
    acc[...] = jnp.zeros_like(acc)
    for copy in got_inner + got_outer:
        copy.wait()

    def inner_weight(f):
        return pool[EARLY + f].reshape(D, FFT)

    def outer_weight(f):
        return w_outer[f].reshape(FFT, D)

    def feed(f, carry):
        cols = pl.ds(pl.multiple_of(f * FFT, FFT), FFT)
        pre = dot(low1[...].reshape(tokens, D), inner_weight(f)) + b_inner[0:1, cols]
        half = 0.5 * (1.0 + lax.erf(pre * (1.0 / math.sqrt(2.0))))
        slope[f] = (half + pre * jnp.exp(-0.5 * pre * pre) * (1.0 / math.sqrt(2.0 * math.pi))).astype(BF)
        act_low = (pre * half).astype(BF)
        act[f] = act_low
        acc[...] += dot(act_low, outer_weight(f)).reshape(3, BLOCK, D)
        return carry

    lax.fori_loop(0, FFN, feed, 0)

    for slot in range(3):
        landed(cotq.at[slot], c_recv.at[slot])
    for u in range(3):
        resid = unit1[u] * gain_first[...] + shift_first[...] + acc[u] + b_outer[...]
        unit, inverse = moments(resid)
        up = cotq[u].astype(F32)
        cotq[u] = (unit * gain_second[...] + shift_second[...]).astype(BF)
        d_second = norm_back(up, unit, inverse, gain_second[...])
        d_low = d_second.astype(BF)
        acc[u] = d_second
        d_out[u] = d_low
        vec[5:6] += column_sum(d_low.astype(F32))
        vec[6:7] += column_sum(up * unit)
        vec[7:8] += column_sum(up)

    row_core = jnp.where(z == 3, 1, 0)
    row_slot = lax.rem(z, 3)
    move.send(cotq.at[0], lay_out.at[row_slot], lay_s.at[0], lay_r.at[row_slot], 2 * c, row_core)
    move.send(cotq.at[1], lay_out.at[row_slot], lay_s.at[1], lay_r.at[row_slot], 2 * c + 1, row_core)
    move.send(cotq.at[2], lay_out.at[1 + deep], lay_s.at[2], lay_r.at[1 + deep], 2 * lowz + c, 1)

    def split(i):
        t = lax.rem(i, 2)
        return t, 1 - t

    def sent_piece(i, e):
        t, s = split(i)
        return 2 * (t * (2 * (1 - by) + e) + s * (2 * e + 1 - bx))

    def kept_piece(i, e):
        t, s = split(i)
        return 2 * (t * (2 * by + e) + s * (2 * e + bx))

    def second_to(i):
        t, s = split(i)
        return at(z, beta + s * (2 - 4 * bx) + t * (4 - 8 * by))

    def third_to(i):
        t, s = split(i)
        return at(z, beta + t * (2 - 4 * bx) + s * (4 - 8 * by))

    def kept_half(i):
        t, s = split(i)
        return t * bx + s * by

    def first_send(i):
        return remote(pool.at[i, pl.ds(8 * (1 - c), 8)], r1.at[i], s1.at[i], t1.at[i], sibling)

    def second_send(i, e):
        return remote(r1.at[i, pl.ds(sent_piece(i, e), 2)], r2.at[i, e], s2.at[i, e], t2.at[i, e], second_to(i))

    def third_send(i):
        return remote(r2.at[i, 1 - kept_half(i)], r3.at[i], s3.at[i], t3.at[i], third_to(i))

    def outer_send(i):
        return remote(r3.at[i], ro.at[i], so.at[i], to.at[i], near)

    def cross_send(i):
        return remote(r3.at[i, 1 - mine], rj.at[i], sj.at[i], tj.at[i], across)

    def final_near(i):
        return remote(sums.at[i, mine], sums.at[i, mine], sf.at[i, 0], tf.at[i, mine], near)

    def final_across(i):
        return remote(sums.at[i, mine], sums.at[i, mine], sf.at[i, 1], tf.at[i, mine], across)

    def final_forward(i):
        return remote(sums.at[i, 1 - mine], sums.at[i, 1 - mine], sf.at[i, 2], tf.at[i, 1 - mine], near)

    def wide(value):
        return value.astype(F32)

    def pair_sum(i, p):
        return wide(r1[i, pl.ds(p, 2)]) + wide(pool[i, pl.ds(8 * c + p, 2)])

    def stage2(i):
        landed(r1.at[i], t1.at[i])
        for order in range(2):
            e = lax.rem(1 - kept_half(i) + order, 2)
            p = sent_piece(i, e)
            r1[i, pl.ds(p, 2)] = pair_sum(i, p).astype(BF)
            second_send(i, e).start()

    def stage3(i):
        e = 1 - kept_half(i)
        landed(r2.at[i, e], t2.at[i, e])
        r2[i, e] = (wide(r2[i, e]) + pair_sum(i, kept_piece(i, e))).astype(BF)
        third_send(i).start()

    def stage4(i):
        e = kept_half(i)
        landed(r2.at[i, e], t2.at[i, e])
        landed(r3.at[i], t3.at[i])
        r3[i] = (wide(r2[i, e]) + pair_sum(i, kept_piece(i, e)) + wide(r3[i])).astype(BF)

        @pl.when(outer)
        def _():
            outer_send(i).start()

    def stage5(i):
        @pl.when(inner)
        def _():
            landed(ro.at[i], to.at[i])
            r3[i, 1 - mine] = (wide(r3[i, 1 - mine]) + wide(ro[i, 1 - mine])).astype(BF)
            cross_send(i).start()

    def stage6(i):
        @pl.when(inner)
        def _():
            landed(rj.at[i], tj.at[i])
            sums[i, mine] = (wide(r3[i, mine]) + wide(ro[i, mine]) + wide(rj[i])).astype(BF)
            final_near(i).start()
            final_across(i).start()

    def stage7(i):
        @pl.when(inner)
        def _():
            landed(sums.at[i, 1 - mine], tf.at[i, 1 - mine])
            final_forward(i).start()

    stages = list(zip((stage2, stage3, stage4, stage5, stage6, stage7), LAGS))

    def tick(n):
        for stage, lag in stages:
            i = n - lag

            @pl.when(jnp.logical_and(i >= 0, i < CHUNKS))
            def _(i=i, stage=stage):
                stage(i)

    up_all = d_out[...].reshape(tokens, D)
    for f in range(FFN):
        g_outer = dot_tn(act[f], up_all).astype(BF)
        for piece in range(2):
            for part in range(4):
                row = 384 * piece + 96 * part
                at_row = 8 * piece + 2 * f
                pool[part, at_row : at_row + 2] = g_outer[row : row + 96].reshape(2, 48, D)
    for i in range(4):
        first_send(i).start()

    def keep_rows(i, grad):
        low_grad = grad.astype(BF)
        for p in range(8):
            at_row = 8 * (p % 2) + 2 * (p // 2)
            pool[i, at_row : at_row + 2] = low_grad[96 * p : 96 * p + 96].reshape(2, 48, D)

    def feed_back(f, carry):
        up = d_out[...].reshape(tokens, D)
        d_pre = (dot_nt(up, outer_weight(f)) * slope[f].astype(F32)).astype(BF)
        vec[pl.ds(8 + f, 1)] = column_sum(d_pre.astype(F32))
        keep_rows(4 + f, dot_tn(low1[...].reshape(tokens, D), d_pre))
        first_send(4 + f).start()
        acc[...] += dot_nt(d_pre, inner_weight(f)).reshape(3, BLOCK, D)
        tick(f)
        return carry

    lax.fori_loop(0, FFN, feed_back, 0)

    for u in range(3):
        up = acc[u]
        d_first = norm_back(up, unit1[u], inv1[u][:, 0:1], gain_first[...])
        acc[u] = d_first
        d_low = d_first.astype(BF)
        d_out[u] = d_low
        vec[2:3] += column_sum(d_low.astype(F32))
        vec[3:4] += column_sum(up * unit1[u])
        vec[4:5] += column_sum(up)
    up_all = d_out[...].reshape(tokens, D)
    keep_rows(8, dot_tn(att[...].reshape(tokens, D), up_all))
    first_send(8).start()
    d_out[...] = dot_nt(up_all, w_out[...]).astype(BF).reshape(3, BLOCK, D)
    tick(FFN)

    def attend_back(j):
        cols = lanes(j)
        for ab in range(2):
            keys, values = k[ab, :, cols], v[ab, :, cols]
            g_key = g_value = None
            for u in (0, 1) if ab == 0 else (2,):
                q_both = stack_heads(q[u, :, cols], low)
                score = dot_nt(q_both, keys)
                score = (score.reshape(2, BLOCK, ROW) + bias[u][None]).reshape(2 * BLOCK, ROW)
                even = jnp.sum(jnp.where(lane == 2 * j, lse[u], 0.0), axis=-1, keepdims=True)
                odd = jnp.sum(jnp.where(lane == 2 * j + 1, lse[u], 0.0), axis=-1, keepdims=True)
                p = jnp.exp(score - jnp.concatenate([even, odd], axis=0))
                d_pair = d_out[u, :, cols]
                d_both = stack_heads(d_pair, low)
                product = wide(d_pair) * wide(att[u, :, cols])
                even = jnp.sum(jnp.where(low, product, 0.0), axis=-1, keepdims=True)
                odd = jnp.sum(jnp.where(low, 0.0, product), axis=-1, keepdims=True)
                d_prob = dot_nt(d_both, values)
                d_score = (p * (d_prob - jnp.concatenate([even, odd], axis=0))).astype(BF)
                one_key = dot(q_both.T, d_score)
                one_value = dot(d_both.T, p.astype(BF))
                g_key = one_key if g_key is None else g_key + one_key
                g_value = one_value if g_value is None else g_value + one_value
                q[u, :, cols] = (merge_heads(dot(d_score, keys), low) * 0.125).astype(BF)
            k[ab, :, cols] = g_key.astype(BF).T
            v[ab, :, cols] = g_value.astype(BF).T

    def step(j, carry):
        attend_back(j)

        @pl.when(lax.rem(j, 2) == 1)
        def _():
            tick(FFN + 1 + j // 2)

        return carry

    lax.fori_loop(0, PAIRS, step, 0)
    done = FFN + 1 + PAIRS // 2

    keep_rows(9, sum(dot_tn(own_tokens(u), q[u]) for u in range(3)))
    first_send(9).start()
    for i, grads in ((10, k), (11, v)):
        keep_rows(i, sum(dot_tn(x[ab].reshape(ROW, D), grads[ab]) for ab in range(2)))
        first_send(i).start()
    tick(done)
    sv[0] = vec[...]
    sv[0, 0:1] = sum(column_sum(wide(q[u])) for u in range(3))
    sv[0, 1:2] = sum(column_sum(wide(v[ab])) for ab in range(2))
    vec_to = [sibling, to_x, to_y, at(z + 1 - 2 * lowz, beta), at(z + 2 - 4 * deep, beta)]

    def vec_send(i):
        return remote(sv.at[i], rv.at[i], vs.at[i], vr.at[i], vec_to[i])

    vec_send(0).start()

    def share(ab, b):
        rows_b = pl.ds(pl.multiple_of(b * BLOCK, BLOCK), BLOCK)
        return dot_nt(k[ab, rows_b, :], w_key[...]) + dot_nt(v[ab, rows_b, :], w_value[...])

    def query_share(u):
        return dot_nt(q[u], w_query[...]) + acc[u]

    def put(ab, b, value):
        x[ab, b] = value.astype(BF).reshape(2, 64, D)

    swap = []
    for e in range(2):
        b = 2 * (1 - c) + e
        put(0, b, share(0, b))
        swap.append(remote(x.at[0, b], rxa.at[e], xs.at[0, e], xr.at[0, e], sibling))
        swap[-1].start()
    for e in range(2):
        b = 1 - c + 2 * e
        put(1, b, share(1, b))
        swap.append(remote(x.at[1, b], rxb.at[e], xs.at[1, e], xr.at[1, e], sibling))
        swap[-1].start()
    tick(done + 1)
    for e in range(2):
        total = share(0, 2 * c + e) + query_share(e)
        landed(rxa.at[e], xr.at[0, e])
        rxa[e] = (total + wide(rxa[e]).reshape(BLOCK, D)).astype(BF).reshape(2, 64, D)
        move.send(rxa.at[e], grad_parts.at[row_slot, 0], gs.at[e], gr.at[row_slot, 0], 2 * c + e, row_core)
    unit1[0] = query_share(2)
    for e in range(2):
        total = share(1, c + 2 * e) + jnp.where(lowz == e, unit1[0], 0.0)
        landed(rxb.at[e], xr.at[1, e])
        rxb[e] = (total + wide(rxb[e]).reshape(BLOCK, D)).astype(BF).reshape(2, 64, D)
        move.send(rxb.at[e], grad_parts.at[1 + deep, lowz], gs.at[2 + e], gr.at[1 + deep, lowz], c + 2 * e, 1)
    done += 2

    def vec_stage(i):
        landed(rv.at[i], vr.at[i])
        total = sv[i] + rv[i]
        if i < 4:
            sv[i + 1] = total
            vec_send(i + 1).start()
        else:
            vec_out[...] = total

    for i in range(5):
        tick(done + i)
        vec_stage(i)
    done += 5

    def rest(n, carry):
        tick(n)
        return carry

    lax.fori_loop(done, CHUNKS + LAGS[-1], rest, 0)

    def close(i, carry):
        first_send(i).wait_send()
        for e in range(2):
            second_send(i, e).wait_send()
        third_send(i).wait_send()

        @pl.when(outer)
        def _():
            outer_send(i).wait_send()
            landed(sums.at[i, 0], tf.at[i, 0])
            landed(sums.at[i, 1], tf.at[i, 1])

        @pl.when(inner)
        def _():
            cross_send(i).wait_send()
            final_near(i).wait_send()
            final_across(i).wait_send()
            final_forward(i).wait_send()

        return carry

    lax.fori_loop(0, CHUNKS, close, 0)
    for i in range(5):
        vec_send(i).wait_send()
    for copy in swap:
        copy.wait_send()
    for slot in range(3):
        landed(lay_out.at[slot], lay_r.at[slot])
        landed(grad_parts.at[slot, 0], gr.at[slot, 0])

    @pl.when(c == 1)
    def _():
        for slot in range(1, 3):
            landed(grad_parts.at[slot, 1], gr.at[slot, 1])

    move.finish()


def whole_layer(tokens, segments, cotangent, weights, vectors):
    vmem, anywhere = pl.BlockSpec(memory_space=pltpu.VMEM), pl.BlockSpec(memory_space=pl.ANY)
    dma = pltpu.SemaphoreType.DMA
    args = (tokens, segments, cotangent) + weights + vectors
    n = CHUNKS
    tok = (3, BLOCK, D)
    square = (16, 48, D)
    buffers = [
        ((EARLY + FFN,) + square, BF),
        ((FFN,) + square, BF),
        ((D, D), BF),
        ((D, D), BF),
        ((D, D), BF),
        ((D, D), BF),
        ((8, D), F32),
        ((8, FFN * FFT), F32),
        ((2, 4, 2, 64, D), BF),
        ((2, 4, 8, BLOCK), jnp.int32),
        (tok, BF),
        (tok, BF),
        ((2, ROW, D), BF),
        ((2, ROW, D), BF),
        (tok, BF),
        (tok, BF),
        ((FFN, 3 * BLOCK, FFT), BF),
        ((FFN, 3 * BLOCK, FFT), BF),
        (tok, F32),
        (tok, F32),
        (tok, BF),
        ((3, BLOCK, ROW), F32),
        ((3, BLOCK, LANES), F32),
        ((3, BLOCK, LANES), F32),
        ((16, D), F32),
        ((n, 8, 48, D), BF),
        ((n, 2, 2, 48, D), BF),
        ((n, 2, 48, D), BF),
        ((n, 2, 48, D), BF),
        ((n, 48, D), BF),
        ((2, 2, 64, D), BF),
        ((2, 2, 64, D), BF),
        ((5, 16, D), F32),
        ((5, 16, D), F32),
    ]
    semaphores = [(21,), (16,), (2, 4, 2), (2, 4), (16,), (2, 4), (6,), (3,)]
    semaphores += [(n,), (n,), (n, 2), (n, 2)] + [(n,)] * 6 + [(n, 3), (n, 2)]
    semaphores += [(3,), (3,), (2, 2), (2, 2), (4,), (3, 2), (5,), (5,)]
    return pl.pallas_call(
        layer_body,
        out_shape=(
            jax.ShapeDtypeStruct((n, 2, 48, D), BF),
            jax.ShapeDtypeStruct((16, D), F32),
            jax.ShapeDtypeStruct(tok, BF),
            jax.ShapeDtypeStruct((3, 2, 2, 64, D), BF),
        ),
        in_specs=[anywhere] * len(args),
        out_specs=[vmem] * 4,
        scratch_shapes=[pltpu.VMEM(s, t) for s, t in buffers] + [dma(s) for s in semaphores],
        compiler_params=pltpu.CompilerParams(
            collective_id=0, has_side_effects=True, vmem_limit_bytes=int(63.9 * MIB)
        ),
    )(*args)


def finish_body(sums, vec, lay, parts, *outs):
    p = lax.rem(lax.axis_index("batch"), 8)
    c = lax.rem(p, 2)
    layer_out, input_grad, g_q, g_k, g_v, g_o, g_inner, g_outer, b_inner = outs[:9]
    layer_out[...] = lay[...]
    input_grad[...] = parts[:, 0].reshape(3, BLOCK, D)

    @pl.when(c == 1)
    def _():
        for slot in range(1, 3):
            both = parts[slot, 0].astype(F32) + parts[slot, 1].astype(F32)
            input_grad[slot] = both.astype(BF).reshape(BLOCK, D)

    def piece(i):
        return sums[i].reshape(96, D).astype(F32)

    for part in range(4):
        g_outer[96 * part : 96 * part + 96] = piece(part)
    for f in range(FFN):
        g_inner[:, f * FFT : (f + 1) * FFT] = piece(4 + f)
    g_o[...] = piece(8)
    g_q[...] = piece(9)
    g_k[...] = piece(10)
    g_v[...] = piece(11)
    pick = lax.broadcasted_iota(jnp.int32, (D, LANES), 0) == lax.broadcasted_iota(jnp.int32, (D, LANES), 1) + 96 * p
    vecs = jnp.dot(
        vec[0:8], pick.astype(F32), preferred_element_type=F32, precision=lax.Precision.HIGHEST
    )
    for i in range(8):
        outs[9 + i][...] = vecs[i, 0:96]
    quarter = vec[pl.ds(8 + p // 2, 1), :]
    b_inner[...] = jnp.where(lax.rem(p, 2) == 0, quarter[:, :384], quarter[:, 384:]).reshape(384)


def finish(sums, vec, lay, parts):
    vmem = pl.BlockSpec(memory_space=pltpu.VMEM)
    tok = (3, BLOCK, D)
    shapes = [
        (tok, BF),
        (tok, BF),
        ((96, D), F32),
        ((96, D), F32),
        ((96, D), F32),
        ((96, D), F32),
        ((96, 4 * D), F32),
        ((384, D), F32),
        ((384,), F32),
    ] + [((96,), F32)] * 8
    return pl.pallas_call(
        finish_body,
        out_shape=tuple(jax.ShapeDtypeStruct(s, t) for s, t in shapes),
        in_specs=[vmem] * 4,
        out_specs=[vmem] * len(shapes),
        compiler_params=pltpu.CompilerParams(vmem_limit_bytes=60 * MIB),
    )(sums, vec, lay, parts)


def per_device(
    groups,
    tokens,
    segment_ids,
    w_query,
    b_query,
    w_key,
    w_value,
    b_value,
    w_out,
    b_out,
    gain_first,
    shift_first,
    w_inner,
    b_inner,
    w_outer,
    b_outer,
    gain_second,
    shift_second,
    cotangent,
):
    weights = (w_query, w_key, w_value, w_out, w_inner.reshape(16, 48, FFN * FFT), w_outer.reshape(FFN, 16, 48, D))
    vectors = (b_query, b_value, b_out, gain_first, shift_first, b_outer, gain_second, shift_second, b_inner)
    reduced = whole_layer(tokens.reshape(3, 2, 64, D), segment_ids, cotangent, weights, vectors)
    layer_out, input_grad, g_q, g_k, g_v, g_o, g_inner, g_outer, g_b_inner, *vecs = finish(*reduced)
    g_b_query, g_b_value, g_b_out, g_gain_first, g_shift_first, g_b_outer, g_gain_second, g_shift_second = vecs
    grads = (
        g_q,
        g_b_query,
        g_k,
        g_v,
        g_b_value,
        g_o,
        g_b_out,
        g_gain_first,
        g_shift_first,
        g_inner,
        g_b_inner,
        g_outer,
        g_b_outer,
        g_gain_second,
        g_shift_second,
    )
    if groups > 1:
        place_at = lax.rem(lax.axis_index("batch"), 8)

        def spread(grad):
            whole = jnp.zeros((8 * grad.shape[0],) + grad.shape[1:], grad.dtype)
            whole = lax.dynamic_update_slice_in_dim(whole, grad, place_at * grad.shape[0], 0)
            return lax.psum_scatter(whole, "batch", scatter_dimension=0, tiled=True)

        grads = tuple(spread(grad) for grad in grads)
    return (layer_out, input_grad) + grads


def solution(mesh):
    tokens = P("batch", "blk", None)
    weight, vector = P("batch", None), P("batch")
    return jax.shard_map(
        functools.partial(per_device, mesh.shape["batch"] // 8),
        mesh=mesh,
        in_specs=(tokens, P("batch", "blk")) + (P(),) * 15 + (tokens,),
        out_specs=(tokens, tokens)
        + (
            weight,
            vector,
            weight,
            weight,
            vector,
            weight,
            vector,
            vector,
            vector,
            weight,
            vector,
            weight,
            vector,
            vector,
            vector,
        ),
        check_vma=False,
    )
```

time: 226 us -> 164 us (0.73)
  Pallas kernels: 203 us -> 163 us
  local copies, waits for them, and re-layouts: 20.7 us -> 0 us
    pallas_call x3 -> x1, Pallas kernels: 200 us -> 158 us  [whole_layer(): pl.pallas_call(layer_body, out_shape=(jax.ShapeDtypeStruct((n, 2, 48, D),...]
    reshape x8 -> x0, local copies, waits for them, and re-layouts: 10.2 us -> none  [row(): return value.reshape(1, -1)]
    unnamed x18 -> x0, local copies, waits for them, and re-layouts: 9.34 us -> none
where the time goes in v2:
time: 164 us; the launch traced here: 163 us
  Pallas kernels  163 us (99%)
    pallas_call x1, Pallas kernels, whole_layer(): pl.pallas_call(layer_body, out_shape=(jax.ShapeDtypeStruct((n, 2, 48, D),...  158 us
    pallas_call x1, Pallas kernels, finish(): pl.pallas_call(finish_body, out_shape=tuple((jax.ShapeDtypeStruct(s, t) f...  4.31 us

profile of v2, /device:TPU:0, one launch (start us, length us, event | category | flops | bytes accessed | tf_op | source)
XLA Modules:
  0.0 163.4 jit_solution(15931172950518938442)
XLA Ops:
  0.7 158.2 %shard_map.305 = (bf16[12,2,48,768]{3,2,1,0:T(8,128)(2,1)}, f32[16,768]{1,0:T(8,128)}, bf16[3,128,768]{2,1,0:T(8,128)(2,1)}, bf16[3,2,2,64,768]{4,3,2,1,0:T(8,128)(2,1)}) custom-call(bf16[3,2,64,768]{3,2,1,0:T(8,128)(2,1)} %bitcast.5, s32[3,128]{1,0:T(4,128)} %seg.1, bf16[3,128,768]{2,1,0:T(8,128)(2,1)} %cot.1, bf16[768,768]{1,0:T(8,128)(2,1)} %w_query_in.1, ...), custom_call_target="tpu_custom_call" | custom-call | tf_op jit(solution)/shard_map/pallas_call | solution.py:749
  158.9 4.3 %shard_map.306 = (bf16[3,128,768]{2,1,0:T(8,128)(2,1)}, bf16[3,128,768]{2,1,0:T(8,128)(2,1)}, f32[96,768]{1,0:T(8,128)}, f32[96,768]{1,0:T(8,128)}, f32[96,768]{...) custom-call(bf16[12,2,48,768]{3,2,1,0:T(8,128)(2,1)} %get-tuple-elem, ...), custom_call_target="tpu_custom_call" | custom-call | tf_op jit(solution)/shard_map/pallas_call | solution.py:814

commit v3 on v2

--- a/solution.py
+++ b/solution.py
@@ -19,8 +19,8 @@
 FFT = 768
 FFN = 4
 EARLY = 9
-CHUNKS = 12
-LAGS = (0, 2, 4, 5, 6, 7)
+CHUNKS = 24
+LAGS = (0, 2, 4, 7, 10, 13)
 MIB = 1 << 20
 
 
@@ -211,7 +211,6 @@
     t3,
     so,
     to,
-    sj,
     tj,
     sf,
     tf,
@@ -232,7 +231,6 @@
     to_x, to_y = at(z, beta + 2 - 4 * bx), at(z, beta + 4 - 8 * by)
     inner = jnp.logical_and(z > 0, z < 3)
     outer = jnp.logical_not(inner)
-    mine = jnp.where(z == 2, 1, 0)
     near = at(jnp.where(z < 2, 1 - z, 5 - z), beta)
     across = at(jnp.where(z == 1, 2, 1), beta)
     deep, lowz = z // 2, lax.rem(z, 2)
@@ -255,15 +253,19 @@
         (2, 1, 2, second),
         (2, 1, 3, second),
     ]
-    count = 0
-    for slot, ab, chip, when in routes:
-        for half in range(2):
-            move.send(
-                tok.at[slot, half], x.at[ab, z, half], d_send.at[count], d_recv.at[ab, z, half], chip, half, when
-            )
-            move.send(seg.at[slot], segs.at[ab, z, 0], g_send.at[count], g_recv.at[ab, z], chip, half, when)
-            count += 1
-
+    counts = iter(range(16))
+
+    def send_rows(which):
+        for slot, ab, chip, when in routes:
+            if ab == which:
+                for half in range(2):
+                    n = next(counts)
+                    move.send(
+                        tok.at[slot, half], x.at[ab, z, half], d_send.at[n], d_recv.at[ab, z, half], chip, half, when
+                    )
+                    move.send(seg.at[slot], segs.at[ab, z, 0], g_send.at[n], g_recv.at[ab, z], chip, half, when)
+
+    send_rows(0)
     got_key = load(w_key_in, w_key)
     got_value = load(w_value_in, w_value)
     got_query = load(w_query_in, w_query)
@@ -279,19 +281,23 @@
     )
     vec[...] = jnp.zeros_like(vec)
     forwards = []
-    for ab in range(2):
+
+    def forward_rows(ab):
         for b in range(4):
             landed(x.at[ab, b, c], d_recv.at[ab, b, c])
             copy = remote(x.at[ab, b, c], x.at[ab, b, c], f_send.at[ab, b], d_recv.at[ab, b, c], sibling)
             copy.start()
             forwards.append(copy)
 
-    for slot in range(3):
-        move.send(cot.at[slot], cotq.at[lowz], c_send.at[slot], c_recv.at[lowz], slot, deep, first)
-    move.send(cot.at[0], cotq.at[lowz], c_send.at[3], c_recv.at[lowz], 3, deep, second)
-    move.send(cot.at[1], cotq.at[2], c_send.at[4], c_recv.at[2], deep, lowz, second)
-    move.send(cot.at[2], cotq.at[2], c_send.at[5], c_recv.at[2], 2 + deep, lowz, second)
-
+    def send_cotangents():
+        for slot in range(3):
+            move.send(cot.at[slot], cotq.at[lowz], c_send.at[slot], c_recv.at[lowz], slot, deep, first)
+        move.send(cot.at[0], cotq.at[lowz], c_send.at[3], c_recv.at[lowz], 3, deep, second)
+        move.send(cot.at[1], cotq.at[2], c_send.at[4], c_recv.at[2], deep, lowz, second)
+        move.send(cot.at[2], cotq.at[2], c_send.at[5], c_recv.at[2], 2 + deep, lowz, second)
+
+    forward_rows(0)
+    send_rows(1)
     own_blocks = [(0, 2 * c), (0, 2 * c + 1), (1, 2 * lowz + c)]
 
     def own_tokens(u):
@@ -306,7 +312,7 @@
     got_query.wait()
     for copy in got_rows:
         copy.wait()
-    for ab in range(2):
+    def project(ab):
         for b in range(4):
             landed(x.at[ab, b, 1 - c], d_recv.at[ab, b, 1 - c])
             landed(segs.at[ab, b, 0], g_recv.at[ab, b])
@@ -343,10 +349,15 @@
         att[u, :, cols] = merge_heads(dot(p, v[ab, :, cols]), low).astype(BF)
         return carry
 
+    lse[...] = jnp.zeros_like(lse)
+    project(0)
+    lax.fori_loop(0, 2 * PAIRS, attend, 0)
+    forward_rows(1)
+    send_cotangents()
+    project(1)
     for copy in forwards:
         copy.wait_send()
-    lse[...] = jnp.zeros_like(lse)
-    lax.fori_loop(0, 3 * PAIRS, attend, 0)
+    lax.fori_loop(2 * PAIRS, 3 * PAIRS, attend, 0)
 
     got_out.wait()
     acc[...] = dot(att[...].reshape(tokens, D), w_out[...]).reshape(3, BLOCK, D)
@@ -405,11 +416,11 @@
 
     def sent_piece(i, e):
         t, s = split(i)
-        return 2 * (t * (2 * (1 - by) + e) + s * (2 * e + 1 - bx))
+        return t * (2 * (1 - by) + e) + s * (2 * e + 1 - bx)
 
     def kept_piece(i, e):
         t, s = split(i)
-        return 2 * (t * (2 * by + e) + s * (2 * e + bx))
+        return t * (2 * by + e) + s * (2 * e + bx)
 
     def second_to(i):
         t, s = split(i)
@@ -423,11 +434,21 @@
         t, s = split(i)
         return t * bx + s * by
 
+    def finisher(i):
+        return z == 1 + lax.rem(i // 2, 2)
+
+    def helper(i):
+        return z == 2 - lax.rem(i // 2, 2)
+
+    def place_in(i):
+        return i // 2, 8 * lax.rem(i, 2)
+
     def first_send(i):
-        return remote(pool.at[i, pl.ds(8 * (1 - c), 8)], r1.at[i], s1.at[i], t1.at[i], sibling)
+        chunk, row = place_in(i)
+        return remote(pool.at[chunk, pl.ds(row + 4 * (1 - c), 4)], r1.at[i], s1.at[i], t1.at[i], sibling)
 
     def second_send(i, e):
-        return remote(r1.at[i, pl.ds(sent_piece(i, e), 2)], r2.at[i, e], s2.at[i, e], t2.at[i, e], second_to(i))
+        return remote(r1.at[i, sent_piece(i, e)], r2.at[i, e], s2.at[i, e], t2.at[i, e], second_to(i))
 
     def third_send(i):
         return remote(r2.at[i, 1 - kept_half(i)], r3.at[i], s3.at[i], t3.at[i], third_to(i))
@@ -435,30 +456,31 @@
     def outer_send(i):
         return remote(r3.at[i], ro.at[i], so.at[i], to.at[i], near)
 
+    def crossed(i):
+        return 2 * (i // 4) + lax.rem(i, 2)
+
     def cross_send(i):
-        return remote(r3.at[i, 1 - mine], rj.at[i], sj.at[i], tj.at[i], across)
+        return remote(r3.at[i], rj.at[crossed(i)], so.at[i], tj.at[crossed(i)], across)
 
     def final_near(i):
-        return remote(sums.at[i, mine], sums.at[i, mine], sf.at[i, 0], tf.at[i, mine], near)
+        return remote(sums.at[i], sums.at[i], sf.at[i, 0], tf.at[i], near)
 
     def final_across(i):
-        return remote(sums.at[i, mine], sums.at[i, mine], sf.at[i, 1], tf.at[i, mine], across)
-
-    def final_forward(i):
-        return remote(sums.at[i, 1 - mine], sums.at[i, 1 - mine], sf.at[i, 2], tf.at[i, 1 - mine], near)
+        return remote(sums.at[i], sums.at[i], sf.at[i, 1], tf.at[i], across)
 
     def wide(value):
         return value.astype(F32)
 
     def pair_sum(i, p):
-        return wide(r1[i, pl.ds(p, 2)]) + wide(pool[i, pl.ds(8 * c + p, 2)])
+        chunk, row = place_in(i)
+        return wide(r1[i, p]) + wide(pool[chunk, row + 4 * c + p])
 
     def stage2(i):
         landed(r1.at[i], t1.at[i])
         for order in range(2):
             e = lax.rem(1 - kept_half(i) + order, 2)
             p = sent_piece(i, e)
-            r1[i, pl.ds(p, 2)] = pair_sum(i, p).astype(BF)
+            r1[i, p] = pair_sum(i, p).astype(BF)
             second_send(i, e).start()
 
     def stage3(i):
@@ -478,25 +500,26 @@
             outer_send(i).start()
 
     def stage5(i):
-        @pl.when(inner)
+        @pl.when(helper(i))
         def _():
             landed(ro.at[i], to.at[i])
-            r3[i, 1 - mine] = (wide(r3[i, 1 - mine]) + wide(ro[i, 1 - mine])).astype(BF)
+            r3[i] = (wide(r3[i]) + wide(ro[i])).astype(BF)
             cross_send(i).start()
 
     def stage6(i):
-        @pl.when(inner)
+        @pl.when(finisher(i))
         def _():
-            landed(rj.at[i], tj.at[i])
-            sums[i, mine] = (wide(r3[i, mine]) + wide(ro[i, mine]) + wide(rj[i])).astype(BF)
+            landed(ro.at[i], to.at[i])
+            landed(rj.at[crossed(i)], tj.at[crossed(i)])
+            sums[i] = (wide(r3[i]) + wide(ro[i]) + wide(rj[crossed(i)])).astype(BF)
             final_near(i).start()
             final_across(i).start()
 
     def stage7(i):
-        @pl.when(inner)
+        @pl.when(helper(i))
         def _():
-            landed(sums.at[i, 1 - mine], tf.at[i, 1 - mine])
-            final_forward(i).start()
+            landed(sums.at[i], tf.at[i])
+            final_near(i).start()
 
     stages = list(zip((stage2, stage3, stage4, stage5, stage6, stage7), LAGS))
 
@@ -513,24 +536,26 @@
         g_outer = dot_tn(act[f], up_all).astype(BF)
         for piece in range(2):
             for part in range(4):
-                row = 384 * piece + 96 * part
-                at_row = 8 * piece + 2 * f
-                pool[part, at_row : at_row + 2] = g_outer[row : row + 96].reshape(2, 48, D)
-    for i in range(4):
+                for half in range(2):
+                    row = 384 * piece + 96 * part + 48 * half
+                    pool[part, 8 * half + 4 * piece + f] = g_outer[row : row + 48]
+    for i in range(8):
         first_send(i).start()
 
     def keep_rows(i, grad):
         low_grad = grad.astype(BF)
         for p in range(8):
-            at_row = 8 * (p % 2) + 2 * (p // 2)
-            pool[i, at_row : at_row + 2] = low_grad[96 * p : 96 * p + 96].reshape(2, 48, D)
+            for half in range(2):
+                row = 96 * p + 48 * half
+                pool[i, 8 * half + 4 * (p % 2) + p // 2] = low_grad[row : row + 48]
+        for half in range(2):
+            first_send(2 * i + half).start()
 
     def feed_back(f, carry):
         up = d_out[...].reshape(tokens, D)
         d_pre = (dot_nt(up, outer_weight(f)) * slope[f].astype(F32)).astype(BF)
         vec[pl.ds(8 + f, 1)] = column_sum(d_pre.astype(F32))
         keep_rows(4 + f, dot_tn(low1[...].reshape(tokens, D), d_pre))
-        first_send(4 + f).start()
         acc[...] += dot_nt(d_pre, inner_weight(f)).reshape(3, BLOCK, D)
         tick(f)
         return carry
@@ -548,7 +573,6 @@
         vec[4:5] += column_sum(up)
     up_all = d_out[...].reshape(tokens, D)
     keep_rows(8, dot_tn(att[...].reshape(tokens, D), up_all))
-    first_send(8).start()
     d_out[...] = dot_nt(up_all, w_out[...]).astype(BF).reshape(3, BLOCK, D)
     tick(FFN)
 
@@ -582,21 +606,18 @@
     def step(j, carry):
         attend_back(j)
 
-        @pl.when(lax.rem(j, 2) == 1)
-        def _():
-            tick(FFN + 1 + j // 2)
-
+        tick(FFN + 1 + j)
         return carry
 
     lax.fori_loop(0, PAIRS, step, 0)
-    done = FFN + 1 + PAIRS // 2
+    done = FFN + 1 + PAIRS
 
     keep_rows(9, sum(dot_tn(own_tokens(u), q[u]) for u in range(3)))
-    first_send(9).start()
+    tick(done)
     for i, grads in ((10, k), (11, v)):
         keep_rows(i, sum(dot_tn(x[ab].reshape(ROW, D), grads[ab]) for ab in range(2)))
-        first_send(i).start()
-    tick(done)
+        tick(done + i - 9)
+    done += 2
     sv[0] = vec[...]
     sv[0, 0:1] = sum(column_sum(wide(q[u])) for u in range(3))
     sv[0, 1:2] = sum(column_sum(wide(v[ab])) for ab in range(2))
@@ -671,15 +692,19 @@
         @pl.when(outer)
         def _():
             outer_send(i).wait_send()
-            landed(sums.at[i, 0], tf.at[i, 0])
-            landed(sums.at[i, 1], tf.at[i, 1])
+            landed(sums.at[i], tf.at[i])
 
         @pl.when(inner)
         def _():
+            final_near(i).wait_send()
+
+        @pl.when(finisher(i))
+        def _():
+            final_across(i).wait_send()
+
+        @pl.when(helper(i))
+        def _():
             cross_send(i).wait_send()
-            final_near(i).wait_send()
-            final_across(i).wait_send()
-            final_forward(i).wait_send()
 
         return carry
 
@@ -733,23 +758,23 @@
         ((3, BLOCK, LANES), F32),
         ((3, BLOCK, LANES), F32),
         ((16, D), F32),
-        ((n, 8, 48, D), BF),
-        ((n, 2, 2, 48, D), BF),
-        ((n, 2, 48, D), BF),
+        ((n, 4, 48, D), BF),
         ((n, 2, 48, D), BF),
         ((n, 48, D), BF),
+        ((n, 48, D), BF),
+        ((n // 2, 48, D), BF),
         ((2, 2, 64, D), BF),
         ((2, 2, 64, D), BF),
         ((5, 16, D), F32),
         ((5, 16, D), F32),
     ]
     semaphores = [(21,), (16,), (2, 4, 2), (2, 4), (16,), (2, 4), (6,), (3,)]
-    semaphores += [(n,), (n,), (n, 2), (n, 2)] + [(n,)] * 6 + [(n, 3), (n, 2)]
+    semaphores += [(n,), (n,), (n, 2), (n, 2)] + [(n,)] * 4 + [(n // 2,), (n, 2), (n,)]
     semaphores += [(3,), (3,), (2, 2), (2, 2), (4,), (3, 2), (5,), (5,)]
     return pl.pallas_call(
         layer_body,
         out_shape=(
-            jax.ShapeDtypeStruct((n, 2, 48, D), BF),
+            jax.ShapeDtypeStruct((n, 48, D), BF),
             jax.ShapeDtypeStruct((16, D), F32),
             jax.ShapeDtypeStruct(tok, BF),
             jax.ShapeDtypeStruct((3, 2, 2, 64, D), BF),
@@ -777,7 +802,7 @@
             input_grad[slot] = both.astype(BF).reshape(BLOCK, D)
 
     def piece(i):
-        return sums[i].reshape(96, D).astype(F32)
+        return sums[2 * i : 2 * i + 2].reshape(96, D).astype(F32)
 
     for part in range(4):
         g_outer[96 * part : 96 * part + 96] = piece(part)

time: 164 us -> 151 us (0.921)
  Pallas kernels: 163 us -> 150 us
    pallas_call x1, Pallas kernels: 158 us -> 146 us  [whole_layer(): pl.pallas_call(layer_body, out_shape=(jax.ShapeDtypeStruct((n, 48, D), BF...]
where the time goes in v3:
time: 151 us
  Pallas kernels  150 us (99%)
    pallas_call x1, Pallas kernels, whole_layer(): pl.pallas_call(layer_body, out_shape=(jax.ShapeDtypeStruct((n, 48, D), BF...  146 us
    pallas_call x1, Pallas kernels, finish(): pl.pallas_call(finish_body, out_shape=tuple((jax.ShapeDtypeStruct(s, t) f...  4.31 us

profile of v3, /device:TPU:0, one launch (start us, length us, event | category | flops | bytes accessed | tf_op | source)
XLA Modules:
  0.0 151.2 jit_solution(9187472988526529899)
XLA Ops:
  0.7 146.1 %shard_map.305 = (bf16[24,48,768]{2,1,0:T(8,128)(2,1)}, f32[16,768]{1,0:T(8,128)}, bf16[3,128,768]{2,1,0:T(8,128)(2,1)}, bf16[3,2,2,64,768]{4,3,2,1,0:T(8,128)(2,1)}) custom-call(bf16[3,2,64,768]{3,2,1,0:T(8,128)(2,1)} %bitcast.5, s32[3,128]{1,0:T(4,128)} %seg.1, bf16[3,128,768]{2,1,0:T(8,128)(2,1)} %cot.1, bf16[768,768]{1,0:T(8,128)(2,1)} %w_query_in.1, ...), custom_call_target="tpu_custom_call" | custom-call | tf_op jit(solution)/shard_map/pallas_call | solution.py:774
  146.7 4.3 %shard_map.306 = (bf16[3,128,768]{2,1,0:T(8,128)(2,1)}, bf16[3,128,768]{2,1,0:T(8,128)(2,1)}, f32[96,768]{1,0:T(8,128)}, f32[96,768]{1,0:T(8,128)}, f32[96,768]{...) custom-call(bf16[24,48,768]{2,1,0:T(8,128)(2,1)} %get-tuple-element., ...), custom_call_target="tpu_custom_call" | custom-call | tf_op jit(solution)/shard_map/pallas_call | solution.py:839

commit v4 on v3

--- a/solution.py
+++ b/solution.py
@@ -20,7 +20,15 @@
 FFN = 4
 EARLY = 9
 CHUNKS = 24
-LAGS = (0, 2, 4, 7, 10, 13)
+ORDER = "".join(
+    (
+        "BF2Y2Y2FW32F3F2Y43L3224A34A3452A34552A643A53645A56W5646X7262",
+        "7264WT33T7277752WO4352T72T52q323k3244vV536246344V56363527573",
+        "6V5274247554643V67562546677336746V37755745764455667667777",
+    )
+)
+KINDS = "234567BFLAXTWOqkvYV"
+LOOPED = "FAT"
 MIB = 1 << 20
 
 
@@ -192,7 +200,6 @@
     ro,
     rj,
     rxa,
-    rxb,
     sv,
     rv,
     w_sem,
@@ -406,42 +413,29 @@
 
     row_core = jnp.where(z == 3, 1, 0)
     row_slot = lax.rem(z, 3)
-    move.send(cotq.at[0], lay_out.at[row_slot], lay_s.at[0], lay_r.at[row_slot], 2 * c, row_core)
-    move.send(cotq.at[1], lay_out.at[row_slot], lay_s.at[1], lay_r.at[row_slot], 2 * c + 1, row_core)
-    move.send(cotq.at[2], lay_out.at[1 + deep], lay_s.at[2], lay_r.at[1 + deep], 2 * lowz + c, 1)
-
-    def split(i):
-        t = lax.rem(i, 2)
-        return t, 1 - t
-
     def sent_piece(i, e):
-        t, s = split(i)
-        return t * (2 * (1 - by) + e) + s * (2 * e + 1 - bx)
+        return 2 * (1 - by) + e if i % 2 else 2 * e + 1 - bx
 
     def kept_piece(i, e):
-        t, s = split(i)
-        return t * (2 * by + e) + s * (2 * e + bx)
+        return 2 * by + e if i % 2 else 2 * e + bx
 
     def second_to(i):
-        t, s = split(i)
-        return at(z, beta + s * (2 - 4 * bx) + t * (4 - 8 * by))
+        return to_y if i % 2 else to_x
 
     def third_to(i):
-        t, s = split(i)
-        return at(z, beta + t * (2 - 4 * bx) + s * (4 - 8 * by))
+        return to_x if i % 2 else to_y
 
     def kept_half(i):
-        t, s = split(i)
-        return t * bx + s * by
+        return bx if i % 2 else by
 
     def finisher(i):
-        return z == 1 + lax.rem(i // 2, 2)
+        return z == 1 + (i // 2) % 2
 
     def helper(i):
-        return z == 2 - lax.rem(i // 2, 2)
+        return z == 2 - (i // 2) % 2
 
     def place_in(i):
-        return i // 2, 8 * lax.rem(i, 2)
+        return i // 2, 8 * (i % 2)
 
     def first_send(i):
         chunk, row = place_in(i)
@@ -457,7 +451,7 @@
         return remote(r3.at[i], ro.at[i], so.at[i], to.at[i], near)
 
     def crossed(i):
-        return 2 * (i // 4) + lax.rem(i, 2)
+        return 2 * (i // 4) + i % 2
 
     def cross_send(i):
         return remote(r3.at[i], rj.at[crossed(i)], so.at[i], tj.at[crossed(i)], across)
@@ -521,26 +515,17 @@
             landed(sums.at[i], tf.at[i])
             final_near(i).start()
 
-    stages = list(zip((stage2, stage3, stage4, stage5, stage6, stage7), LAGS))
-
-    def tick(n):
-        for stage, lag in stages:
-            i = n - lag
-
-            @pl.when(jnp.logical_and(i >= 0, i < CHUNKS))
-            def _(i=i, stage=stage):
-                stage(i)
-
-    up_all = d_out[...].reshape(tokens, D)
-    for f in range(FFN):
-        g_outer = dot_tn(act[f], up_all).astype(BF)
-        for piece in range(2):
-            for part in range(4):
-                for half in range(2):
-                    row = 384 * piece + 96 * part + 48 * half
-                    pool[part, 8 * half + 4 * piece + f] = g_outer[row : row + 48]
-    for i in range(8):
-        first_send(i).start()
+    def block_outer(i):
+        up = d_out[...].reshape(tokens, D)
+        for f in range(FFN):
+            g_outer = dot_tn(act[f], up).astype(BF)
+            for piece in range(2):
+                for part in range(4):
+                    for half in range(2):
+                        row = 384 * piece + 96 * part + 48 * half
+                        pool[part, 8 * half + 4 * piece + f] = g_outer[row : row + 48]
+        for n in range(8):
+            first_send(n).start()
 
     def keep_rows(i, grad):
         low_grad = grad.astype(BF)
@@ -551,32 +536,32 @@
         for half in range(2):
             first_send(2 * i + half).start()
 
-    def feed_back(f, carry):
+    def block_feed(f):
         up = d_out[...].reshape(tokens, D)
         d_pre = (dot_nt(up, outer_weight(f)) * slope[f].astype(F32)).astype(BF)
+        slope[f] = d_pre
         vec[pl.ds(8 + f, 1)] = column_sum(d_pre.astype(F32))
-        keep_rows(4 + f, dot_tn(low1[...].reshape(tokens, D), d_pre))
         acc[...] += dot_nt(d_pre, inner_weight(f)).reshape(3, BLOCK, D)
-        tick(f)
-        return carry
-
-    lax.fori_loop(0, FFN, feed_back, 0)
-
-    for u in range(3):
-        up = acc[u]
-        d_first = norm_back(up, unit1[u], inv1[u][:, 0:1], gain_first[...])
-        acc[u] = d_first
-        d_low = d_first.astype(BF)
-        d_out[u] = d_low
-        vec[2:3] += column_sum(d_low.astype(F32))
-        vec[3:4] += column_sum(up * unit1[u])
-        vec[4:5] += column_sum(up)
-    up_all = d_out[...].reshape(tokens, D)
-    keep_rows(8, dot_tn(att[...].reshape(tokens, D), up_all))
-    d_out[...] = dot_nt(up_all, w_out[...]).astype(BF).reshape(3, BLOCK, D)
-    tick(FFN)
-
-    def attend_back(j):
+
+    def block_inner(f):
+        keep_rows(4 + f, dot_tn(low1[...].reshape(tokens, D), slope[f]))
+
+    def block_norm(i):
+        for u in range(3):
+            up = acc[u]
+            d_first = norm_back(up, unit1[u], inv1[u][:, 0:1], gain_first[...])
+            acc[u] = d_first
+            d_low = d_first.astype(BF)
+            d_out[u] = d_low
+            vec[2:3] += column_sum(d_low.astype(F32))
+            vec[3:4] += column_sum(up * unit1[u])
+            vec[4:5] += column_sum(up)
+        act[0] = dot_nt(d_out[...].reshape(tokens, D), w_out[...]).astype(BF)
+
+    def block_out(i):
+        keep_rows(8, dot_tn(att[...].reshape(tokens, D), d_out[...].reshape(tokens, D)))
+
+    def block_attend(j):
         cols = lanes(j)
         for ab in range(2):
             keys, values = k[ab, :, cols], v[ab, :, cols]
@@ -588,7 +573,7 @@
                 even = jnp.sum(jnp.where(lane == 2 * j, lse[u], 0.0), axis=-1, keepdims=True)
                 odd = jnp.sum(jnp.where(lane == 2 * j + 1, lse[u], 0.0), axis=-1, keepdims=True)
                 p = jnp.exp(score - jnp.concatenate([even, odd], axis=0))
-                d_pair = d_out[u, :, cols]
+                d_pair = act[0, u * BLOCK : (u + 1) * BLOCK, cols]
                 d_both = stack_heads(d_pair, low)
                 product = wide(d_pair) * wide(att[u, :, cols])
                 even = jnp.sum(jnp.where(low, product, 0.0), axis=-1, keepdims=True)
@@ -603,117 +588,173 @@
             k[ab, :, cols] = g_key.astype(BF).T
             v[ab, :, cols] = g_value.astype(BF).T
 
-    def step(j, carry):
-        attend_back(j)
-
-        tick(FFN + 1 + j)
-        return carry
-
-    lax.fori_loop(0, PAIRS, step, 0)
-    done = FFN + 1 + PAIRS
-
-    keep_rows(9, sum(dot_tn(own_tokens(u), q[u]) for u in range(3)))
-    tick(done)
-    for i, grads in ((10, k), (11, v)):
-        keep_rows(i, sum(dot_tn(x[ab].reshape(ROW, D), grads[ab]) for ab in range(2)))
-        tick(done + i - 9)
-    done += 2
-    sv[0] = vec[...]
-    sv[0, 0:1] = sum(column_sum(wide(q[u])) for u in range(3))
-    sv[0, 1:2] = sum(column_sum(wide(v[ab])) for ab in range(2))
-    vec_to = [sibling, to_x, to_y, at(z + 1 - 2 * lowz, beta), at(z + 2 - 4 * deep, beta)]
-
-    def vec_send(i):
-        return remote(sv.at[i], rv.at[i], vs.at[i], vr.at[i], vec_to[i])
-
-    vec_send(0).start()
+    def block_query(i):
+        keep_rows(9, sum(dot_tn(own_tokens(u), q[u]) for u in range(3)))
+
+    def block_key(i):
+        keep_rows(10, sum(dot_tn(x[ab].reshape(ROW, D), k[ab]) for ab in range(2)))
+
+    def block_value(i):
+        keep_rows(11, sum(dot_tn(x[ab].reshape(ROW, D), v[ab]) for ab in range(2)))
 
     def share(ab, b):
         rows_b = pl.ds(pl.multiple_of(b * BLOCK, BLOCK), BLOCK)
         return dot_nt(k[ab, rows_b, :], w_key[...]) + dot_nt(v[ab, rows_b, :], w_value[...])
 
-    def query_share(u):
-        return dot_nt(q[u], w_query[...]) + acc[u]
-
-    def put(ab, b, value):
-        x[ab, b] = value.astype(BF).reshape(2, 64, D)
-
-    swap = []
-    for e in range(2):
-        b = 2 * (1 - c) + e
-        put(0, b, share(0, b))
-        swap.append(remote(x.at[0, b], rxa.at[e], xs.at[0, e], xr.at[0, e], sibling))
-        swap[-1].start()
-    for e in range(2):
-        b = 1 - c + 2 * e
-        put(1, b, share(1, b))
-        swap.append(remote(x.at[1, b], rxb.at[e], xs.at[1, e], xr.at[1, e], sibling))
-        swap[-1].start()
-    tick(done + 1)
-    for e in range(2):
-        total = share(0, 2 * c + e) + query_share(e)
-        landed(rxa.at[e], xr.at[0, e])
-        rxa[e] = (total + wide(rxa[e]).reshape(BLOCK, D)).astype(BF).reshape(2, 64, D)
-        move.send(rxa.at[e], grad_parts.at[row_slot, 0], gs.at[e], gr.at[row_slot, 0], 2 * c + e, row_core)
-    unit1[0] = query_share(2)
-    for e in range(2):
-        total = share(1, c + 2 * e) + jnp.where(lowz == e, unit1[0], 0.0)
-        landed(rxb.at[e], xr.at[1, e])
-        rxb[e] = (total + wide(rxb[e]).reshape(BLOCK, D)).astype(BF).reshape(2, 64, D)
-        move.send(rxb.at[e], grad_parts.at[1 + deep, lowz], gs.at[2 + e], gr.at[1 + deep, lowz], c + 2 * e, 1)
-    done += 2
-
-    def vec_stage(i):
-        landed(rv.at[i], vr.at[i])
-        total = sv[i] + rv[i]
-        if i < 4:
-            sv[i + 1] = total
-            vec_send(i + 1).start()
+    def swap_send(e):
+        src = act.at[1 + e // 2, (e % 2) * BLOCK : (e % 2 + 1) * BLOCK]
+        return remote(src, rxa.at[e], xs.at[e], xr.at[e], sibling)
+
+    def block_swap(i):
+        for e in range(4):
+            b = 2 * (1 - c) + e if e < 2 else 1 - c + 2 * (e - 2)
+            act[1 + e // 2, (e % 2) * BLOCK : (e % 2 + 1) * BLOCK] = share(e // 2, b).astype(BF)
+            swap_send(e).start()
+
+    class Unit:
+        def __init__(self, src, dst, send_sem, recv_sem, to_z, to_c):
+            self.here = jnp.logical_and(to_z == z, to_c == c)
+            self.away = jnp.logical_not(self.here)
+            self.local = pltpu.make_async_copy(src, dst, recv_sem)
+            self.out = remote(src, dst, send_sem, recv_sem, at(to_z, base + to_c))
+
+        def start(self):
+            @pl.when(self.here)
+            def _():
+                self.local.start()
+
+            @pl.when(self.away)
+            def _():
+                self.out.start()
+
+        def finish(self):
+            @pl.when(self.away)
+            def _():
+                self.out.wait_send()
+
+    def layer_unit(u):
+        shared = u // 2
+        slot = (1 - shared) * row_slot + shared * (1 + deep)
+        to_z = (1 - shared) * (2 * c + u) + shared * (2 * lowz + c)
+        to_c = (1 - shared) * row_core + shared
+        return Unit(cotq.at[u], lay_out.at[slot], lay_s.at[u], lay_r.at[slot], to_z, to_c)
+
+    def grad_unit(e):
+        shared = e // 2
+        slot = (1 - shared) * row_slot + shared * (1 + deep)
+        part = shared * lowz
+        to_z = (1 - shared) * (2 * c + e) + shared * (c + 2 * (e - 2))
+        to_c = (1 - shared) * row_core + shared
+        return Unit(rxa.at[e], grad_parts.at[slot, part], gs.at[e], gr.at[slot, part], to_z, to_c)
+
+    def block_layer(u):
+        layer_unit(u).start()
+
+    def block_total(e):
+        shared = e // 2
+        b = (1 - shared) * (2 * c + e) + shared * (c + 2 * (e - 2))
+        own = jnp.logical_or(e < 2, e - 2 == lowz)
+        landed(rxa.at[e], xr.at[e])
+        unit1[0] = share(shared, b) + wide(rxa[e])
+
+        @pl.when(own)
+        def _():
+            u = (1 - shared) * e + shared * 2
+            unit1[0] += dot_nt(q[u], w_query[...]) + acc[u]
+
+        rxa[e] = unit1[0].astype(BF)
+        grad_unit(e).start()
+
+    def vec_send(i):
+        hops = [sibling, to_x, to_y, at(z + 1 - 2 * lowz, beta), at(z + 2 - 4 * deep, beta)]
+        return remote(sv.at[i], rv.at[i], vs.at[i], vr.at[i], hops[i])
+
+    def block_vector(i):
+        if i == 0:
+            sv[0] = vec[...]
+            sv[0, 0:1] = sum(column_sum(wide(q[u])) for u in range(3))
+            sv[0, 1:2] = sum(column_sum(wide(v[ab])) for ab in range(2))
         else:
-            vec_out[...] = total
-
-    for i in range(5):
-        tick(done + i)
-        vec_stage(i)
-    done += 5
-
-    def rest(n, carry):
-        tick(n)
-        return carry
-
-    lax.fori_loop(done, CHUNKS + LAGS[-1], rest, 0)
-
-    def close(i, carry):
+            landed(rv.at[i - 1], vr.at[i - 1])
+            sv[i] = sv[i - 1] + rv[i - 1]
+        vec_send(i).start()
+
+    stages = [stage2, stage3, stage4, stage5, stage6, stage7]
+    blocks = [
+        block_outer,
+        block_feed,
+        block_norm,
+        block_attend,
+        block_swap,
+        block_total,
+        block_inner,
+        block_out,
+        block_query,
+        block_key,
+        block_value,
+        block_layer,
+        block_vector,
+    ]
+    OPS = stages + blocks
+    counts = {kind: 0 for kind in KINDS}
+
+    def emit(kinds):
+        for kind in kinds:
+            OPS[KINDS.index(kind)](counts[kind])
+            counts[kind] += 1
+
+    rest = ORDER
+    for kind in LOOPED:
+        emit(rest[: rest.index(kind)])
+        first_turn, last_turn = rest.index(kind), rest.rindex(kind)
+        between = rest[first_turn + 1 : last_turn].split(kind)
+
+        def turn(n, carry, kind=kind, between=between):
+            OPS[KINDS.index(kind)](n)
+            for at_turn, kinds in enumerate(between):
+
+                @pl.when(n == at_turn)
+                def _(kinds=kinds):
+                    emit(kinds)
+
+            return carry
+
+        lax.fori_loop(0, len(between) + 1, turn, 0)
+        rest = rest[last_turn + 1 :]
+    emit(rest)
+
+    for i in range(CHUNKS):
         first_send(i).wait_send()
         for e in range(2):
             second_send(i, e).wait_send()
         third_send(i).wait_send()
 
         @pl.when(outer)
-        def _():
+        def _(i=i):
             outer_send(i).wait_send()
             landed(sums.at[i], tf.at[i])
 
         @pl.when(inner)
-        def _():
+        def _(i=i):
             final_near(i).wait_send()
 
         @pl.when(finisher(i))
-        def _():
+        def _(i=i):
             final_across(i).wait_send()
 
         @pl.when(helper(i))
-        def _():
+        def _(i=i):
             cross_send(i).wait_send()
 
-        return carry
-
-    lax.fori_loop(0, CHUNKS, close, 0)
+    landed(rv.at[4], vr.at[4])
+    vec_out[...] = sv[4] + rv[4]
     for i in range(5):
         vec_send(i).wait_send()
-    for copy in swap:
-        copy.wait_send()
+    for e in range(4):
+        swap_send(e).wait_send()
+        grad_unit(e).finish()
     for slot in range(3):
+        layer_unit(slot).finish()
         landed(lay_out.at[slot], lay_r.at[slot])
         landed(grad_parts.at[slot, 0], gr.at[slot, 0])
 
@@ -763,21 +804,20 @@
         ((n, 48, D), BF),
         ((n, 48, D), BF),
         ((n // 2, 48, D), BF),
-        ((2, 2, 64, D), BF),
-        ((2, 2, 64, D), BF),
+        ((4, BLOCK, D), BF),
         ((5, 16, D), F32),
         ((5, 16, D), F32),
     ]
     semaphores = [(21,), (16,), (2, 4, 2), (2, 4), (16,), (2, 4), (6,), (3,)]
     semaphores += [(n,), (n,), (n, 2), (n, 2)] + [(n,)] * 4 + [(n // 2,), (n, 2), (n,)]
-    semaphores += [(3,), (3,), (2, 2), (2, 2), (4,), (3, 2), (5,), (5,)]
+    semaphores += [(3,), (3,), (4,), (4,), (4,), (3, 2), (5,), (5,)]
     return pl.pallas_call(
         layer_body,
         out_shape=(
             jax.ShapeDtypeStruct((n, 48, D), BF),
             jax.ShapeDtypeStruct((16, D), F32),
             jax.ShapeDtypeStruct(tok, BF),
-            jax.ShapeDtypeStruct((3, 2, 2, 64, D), BF),
+            jax.ShapeDtypeStruct((3, 2, BLOCK, D), BF),
         ),
         in_specs=[anywhere] * len(args),
         out_specs=[vmem] * 4,
@@ -793,13 +833,13 @@
     c = lax.rem(p, 2)
     layer_out, input_grad, g_q, g_k, g_v, g_o, g_inner, g_outer, b_inner = outs[:9]
     layer_out[...] = lay[...]
-    input_grad[...] = parts[:, 0].reshape(3, BLOCK, D)
+    input_grad[...] = parts[:, 0]
 
     @pl.when(c == 1)
     def _():
         for slot in range(1, 3):
             both = parts[slot, 0].astype(F32) + parts[slot, 1].astype(F32)
-            input_grad[slot] = both.astype(BF).reshape(BLOCK, D)
+            input_grad[slot] = both.astype(BF)
 
     def piece(i):
         return sums[2 * i : 2 * i + 2].reshape(96, D).astype(F32)

time: 151 us -> 141 us (0.934)
  Pallas kernels: 150 us -> 140 us
    pallas_call x1, Pallas kernels: 146 us -> 135 us  [whole_layer(): pl.pallas_call(layer_body, out_shape=(jax.ShapeDtypeStruct((n, 48, D), BF...]
where the time goes in v4:
time: 141 us
  Pallas kernels  140 us (99%)
    pallas_call x1, Pallas kernels, whole_layer(): pl.pallas_call(layer_body, out_shape=(jax.ShapeDtypeStruct((n, 48, D), BF...  135 us
    pallas_call x1, Pallas kernels, finish(): pl.pallas_call(finish_body, out_shape=tuple((jax.ShapeDtypeStruct(s, t) f...  4.31 us

profile of v4, /device:TPU:0, one launch (start us, length us, event | category | flops | bytes accessed | tf_op | source)
XLA Modules:
  0.0 140.6 jit_solution(13004600664392104759)
XLA Ops:
  0.7 135.4 %shard_map.305 = (bf16[24,48,768]{2,1,0:T(8,128)(2,1)}, f32[16,768]{1,0:T(8,128)}, bf16[3,128,768]{2,1,0:T(8,128)(2,1)}, bf16[3,2,128,768]{3,2,1,0:T(8,128)(2,1)}) custom-call(bf16[3,2,64,768]{3,2,1,0:T(8,128)(2,1)} %bitcast.5, s32[3,128]{1,0:T(4,128)} %seg.1, bf16[3,128,768]{2,1,0:T(8,128)(2,1)} %cot.1, bf16[768,768]{1,0:T(8,128)(2,1)} %w_query_in.1, ...), custom_call_target="tpu_custom_call" | custom-call | tf_op jit(solution)/shard_map/pallas_call | solution.py:814
  136.1 4.3 %shard_map.306 = (bf16[3,128,768]{2,1,0:T(8,128)(2,1)}, bf16[3,128,768]{2,1,0:T(8,128)(2,1)}, f32[96,768]{1,0:T(8,128)}, f32[96,768]{1,0:T(8,128)}, f32[96,768]{...) custom-call(bf16[24,48,768]{2,1,0:T(8,128)(2,1)} %get-tuple-element., ...), custom_call_target="tpu_custom_call" | custom-call | tf_op jit(solution)/shard_map/pallas_call | solution.py:879

commit v5 on v4

--- a/solution.py
+++ b/solution.py
@@ -22,12 +22,12 @@
 CHUNKS = 24
 ORDER = "".join(
     (
-        "BF2Y2Y2FW32F3F2Y43L3224A34A3452A34552A643A53645A56W5646X7262",
-        "7264WT33T7277752WO4352T72T52q323k3244vV536246344V56363527573",
-        "6V5274247554643V67562546677336746V37755745764455667667777",
+        "YBF2Y2F22YFF3233L23W342AA42534W24W325A43624535A42563A642565A",
+        "6354X6465W425663T32T2O3q3245T32k25346vV324655436245642563534",
+        "62465256345V64356364V546545V666VT",
     )
 )
-KINDS = "234567BFLAXTWOqkvYV"
+KINDS = "23456BFLAXTWOqkvYV"
 LOOPED = "FAT"
 MIB = 1 << 20
 
@@ -200,6 +200,7 @@
     ro,
     rj,
     rxa,
+    rxb,
     sv,
     rv,
     w_sem,
@@ -227,6 +228,7 @@
     xr,
     gs,
     gr,
+    pr,
     vs,
     vr,
 ):
@@ -289,10 +291,11 @@
     vec[...] = jnp.zeros_like(vec)
     forwards = []
 
-    def forward_rows(ab):
-        for b in range(4):
+    def forward_rows(ab, steps=range(4)):
+        for step in steps:
+            b = (z, z + 1 - 2 * lowz, lax.rem(z + 2, 4), 3 - z)[step]
             landed(x.at[ab, b, c], d_recv.at[ab, b, c])
-            copy = remote(x.at[ab, b, c], x.at[ab, b, c], f_send.at[ab, b], d_recv.at[ab, b, c], sibling)
+            copy = remote(x.at[ab, b, c], x.at[ab, b, c], f_send.at[ab, step], d_recv.at[ab, b, c], sibling)
             copy.start()
             forwards.append(copy)
 
@@ -303,8 +306,9 @@
         move.send(cot.at[1], cotq.at[2], c_send.at[4], c_recv.at[2], deep, lowz, second)
         move.send(cot.at[2], cotq.at[2], c_send.at[5], c_recv.at[2], 2 + deep, lowz, second)
 
-    forward_rows(0)
+    forward_rows(0, range(3))
     send_rows(1)
+    forward_rows(0, range(3, 4))
     own_blocks = [(0, 2 * c), (0, 2 * c + 1), (1, 2 * lowz + c)]
 
     def own_tokens(u):
@@ -339,41 +343,50 @@
 
     lane = lax.broadcasted_iota(jnp.int32, (BLOCK, LANES), 1)
 
-    def scores(u, cols, keys):
-        score = dot_nt(stack_heads(q[u, :, cols], low), keys)
-        return (score.reshape(2, BLOCK, ROW) + bias[u][None]).reshape(2 * BLOCK, ROW)
-
-    def attend(n, carry):
-        u, j = n // PAIRS, lax.rem(n, PAIRS)
-        ab, cols = u // 2, lanes(j)
-        score = scores(u, cols, k[ab, :, cols])
-        top = jnp.max(score, axis=-1, keepdims=True)
-        expo = jnp.exp(score - top)
-        total = jnp.sum(expo, axis=-1, keepdims=True)
-        p = (expo * (1.0 / total)).astype(BF)
-        stat = top + jnp.log(total)
-        lse[u] = jnp.where(lane == 2 * j, stat[:BLOCK], jnp.where(lane == 2 * j + 1, stat[BLOCK:], lse[u]))
-        att[u, :, cols] = merge_heads(dot(p, v[ab, :, cols]), low).astype(BF)
-        return carry
+    def attend(ab, units, start, stop):
+        n, base_u = len(units), units[0]
+
+        def pair(j, carry):
+            cols = lanes(j)
+            both = jnp.concatenate([stack_heads(q[u, :, cols], low) for u in units], axis=0)
+            score = dot_nt(both, k[ab, :, cols]).reshape(n, 2, BLOCK, ROW) + bias[base_u : base_u + n][:, None]
+            score = score.reshape(n * 2 * BLOCK, ROW)
+            top = jnp.max(score, axis=-1, keepdims=True)
+            expo = jnp.exp(score - top)
+            total = jnp.sum(expo, axis=-1, keepdims=True)
+            p = (expo * (1.0 / total)).astype(BF)
+            stat = top + jnp.log(total)
+            heads = dot(p, v[ab, :, cols])
+            for m, u in enumerate(units):
+                even, odd = slice(2 * m * BLOCK, (2 * m + 1) * BLOCK), slice((2 * m + 1) * BLOCK, (2 * m + 2) * BLOCK)
+                lse[u] = jnp.where(lane == 2 * j, stat[even], jnp.where(lane == 2 * j + 1, stat[odd], lse[u]))
+                att[u, :, cols] = jnp.where(low, heads[even], heads[odd]).astype(BF)
+            return carry
+
+        lax.fori_loop(start, stop, pair, 0)
+
+    def out_norm(units):
+        base_u, n = units[0], len(units)
+        acc[base_u : base_u + n] = dot(att[base_u : base_u + n].reshape(n * BLOCK, D), w_out[...]).reshape(n, BLOCK, D)
+        for u in units:
+            resid = own_tokens(u).astype(F32) + acc[u] + b_out[...]
+            unit, inverse = moments(resid)
+            unit1[u] = unit
+            inv1[u] = jnp.broadcast_to(inverse, (BLOCK, LANES))
+            low1[u] = (unit * gain_first[...] + shift_first[...]).astype(BF)
 
     lse[...] = jnp.zeros_like(lse)
     project(0)
-    lax.fori_loop(0, 2 * PAIRS, attend, 0)
+    attend(0, (0, 1), 0, PAIRS)
     forward_rows(1)
     send_cotangents()
+    got_out.wait()
+    out_norm((0, 1))
     project(1)
     for copy in forwards:
         copy.wait_send()
-    lax.fori_loop(2 * PAIRS, 3 * PAIRS, attend, 0)
-
-    got_out.wait()
-    acc[...] = dot(att[...].reshape(tokens, D), w_out[...]).reshape(3, BLOCK, D)
-    for u in range(3):
-        resid = own_tokens(u).astype(F32) + acc[u] + b_out[...]
-        unit, inverse = moments(resid)
-        unit1[u] = unit
-        inv1[u] = jnp.broadcast_to(inverse, (BLOCK, LANES))
-        low1[u] = (unit * gain_first[...] + shift_first[...]).astype(BF)
+    attend(1, (2,), 0, PAIRS)
+    out_norm((2,))
     acc[...] = jnp.zeros_like(acc)
     for copy in got_inner + got_outer:
         copy.wait()
@@ -428,12 +441,6 @@
     def kept_half(i):
         return bx if i % 2 else by
 
-    def finisher(i):
-        return z == 1 + (i // 2) % 2
-
-    def helper(i):
-        return z == 2 - (i // 2) % 2
-
     def place_in(i):
         return i // 2, 8 * (i % 2)
 
@@ -450,17 +457,11 @@
     def outer_send(i):
         return remote(r3.at[i], ro.at[i], so.at[i], to.at[i], near)
 
-    def crossed(i):
-        return 2 * (i // 4) + i % 2
-
     def cross_send(i):
-        return remote(r3.at[i], rj.at[crossed(i)], so.at[i], tj.at[crossed(i)], across)
+        return remote(r3.at[i], rj.at[i], so.at[i], tj.at[i], across)
 
     def final_near(i):
-        return remote(sums.at[i], sums.at[i], sf.at[i, 0], tf.at[i], near)
-
-    def final_across(i):
-        return remote(sums.at[i], sums.at[i], sf.at[i, 1], tf.at[i], across)
+        return remote(sums.at[i], sums.at[i], sf.at[i], tf.at[i], near)
 
     def wide(value):
         return value.astype(F32)
@@ -494,25 +495,17 @@
             outer_send(i).start()
 
     def stage5(i):
-        @pl.when(helper(i))
+        @pl.when(inner)
         def _():
             landed(ro.at[i], to.at[i])
             r3[i] = (wide(r3[i]) + wide(ro[i])).astype(BF)
             cross_send(i).start()
 
     def stage6(i):
-        @pl.when(finisher(i))
+        @pl.when(inner)
         def _():
-            landed(ro.at[i], to.at[i])
-            landed(rj.at[crossed(i)], tj.at[crossed(i)])
-            sums[i] = (wide(r3[i]) + wide(ro[i]) + wide(rj[crossed(i)])).astype(BF)
-            final_near(i).start()
-            final_across(i).start()
-
-    def stage7(i):
-        @pl.when(helper(i))
-        def _():
-            landed(sums.at[i], tf.at[i])
+            landed(rj.at[i], tj.at[i])
+            sums[i] = (wide(r3[i]) + wide(rj[i])).astype(BF)
             final_near(i).start()
 
     def block_outer(i):
@@ -639,31 +632,46 @@
         to_c = (1 - shared) * row_core + shared
         return Unit(cotq.at[u], lay_out.at[slot], lay_s.at[u], lay_r.at[slot], to_z, to_c)
 
-    def grad_unit(e):
-        shared = e // 2
+    def grad_unit(n):
+        shared = n // 2
         slot = (1 - shared) * row_slot + shared * (1 + deep)
-        part = shared * lowz
-        to_z = (1 - shared) * (2 * c + e) + shared * (c + 2 * (e - 2))
+        to_z = (1 - shared) * (2 * c + n) + shared * (c + 2 * lowz)
         to_c = (1 - shared) * row_core + shared
-        return Unit(rxa.at[e], grad_parts.at[slot, part], gs.at[e], gr.at[slot, part], to_z, to_c)
+        src = rxa.at[(1 - shared) * n + shared * (2 + lowz)]
+        return Unit(src, grad_parts.at[slot], gs.at[n], gr.at[slot], to_z, to_c)
+
+    def pair_send():
+        return remote(rxa.at[3 - lowz], rxb, gs.at[2], pr.at[0], at(z + 1 - 2 * lowz, beta))
 
     def block_layer(u):
         layer_unit(u).start()
 
-    def block_total(e):
-        shared = e // 2
-        b = (1 - shared) * (2 * c + e) + shared * (c + 2 * (e - 2))
-        own = jnp.logical_or(e < 2, e - 2 == lowz)
-        landed(rxa.at[e], xr.at[e])
-        unit1[0] = share(shared, b) + wide(rxa[e])
-
-        @pl.when(own)
+    def block_total(n):
+        shared = n // 2
+        e = lax.rem(n + 1 + lowz, 2)
+        at_e = (1 - shared) * n + shared * (2 + e)
+        landed(rxa.at[at_e], xr.at[at_e])
+        unit1[0] = share(shared, (1 - shared) * (2 * c + n) + shared * (c + 2 * e)) + wide(rxa[at_e])
+
+        @pl.when(n != 2)
         def _():
-            u = (1 - shared) * e + shared * 2
+            u = (1 - shared) * n + shared * 2
             unit1[0] += dot_nt(q[u], w_query[...]) + acc[u]
 
-        rxa[e] = unit1[0].astype(BF)
-        grad_unit(e).start()
+        @pl.when(n == 3)
+        def _():
+            landed(rxb, pr.at[0])
+            unit1[0] += wide(rxb[...])
+
+        rxa[at_e] = unit1[0].astype(BF)
+
+        @pl.when(n == 2)
+        def _():
+            pair_send().start()
+
+        @pl.when(n != 2)
+        def _():
+            grad_unit(n).start()
 
     def vec_send(i):
         hops = [sibling, to_x, to_y, at(z + 1 - 2 * lowz, beta), at(z + 2 - 4 * deep, beta)]
@@ -679,7 +687,7 @@
             sv[i] = sv[i - 1] + rv[i - 1]
         vec_send(i).start()
 
-    stages = [stage2, stage3, stage4, stage5, stage6, stage7]
+    stages = [stage2, stage3, stage4, stage5, stage6]
     blocks = [
         block_outer,
         block_feed,
@@ -737,13 +745,6 @@
         @pl.when(inner)
         def _(i=i):
             final_near(i).wait_send()
-
-        @pl.when(finisher(i))
-        def _(i=i):
-            final_across(i).wait_send()
-
-        @pl.when(helper(i))
-        def _(i=i):
             cross_send(i).wait_send()
 
     landed(rv.at[4], vr.at[4])
@@ -752,16 +753,13 @@
         vec_send(i).wait_send()
     for e in range(4):
         swap_send(e).wait_send()
-        grad_unit(e).finish()
+    pair_send().wait_send()
+    for n in (0, 1, 3):
+        grad_unit(n).finish()
     for slot in range(3):
         layer_unit(slot).finish()
         landed(lay_out.at[slot], lay_r.at[slot])
-        landed(grad_parts.at[slot, 0], gr.at[slot, 0])
-
-    @pl.when(c == 1)
-    def _():
-        for slot in range(1, 3):
-            landed(grad_parts.at[slot, 1], gr.at[slot, 1])
+        landed(grad_parts.at[slot], gr.at[slot])
 
     move.finish()
 
@@ -803,21 +801,22 @@
         ((n, 2, 48, D), BF),
         ((n, 48, D), BF),
         ((n, 48, D), BF),
-        ((n // 2, 48, D), BF),
+        ((n, 48, D), BF),
         ((4, BLOCK, D), BF),
+        ((BLOCK, D), BF),
         ((5, 16, D), F32),
         ((5, 16, D), F32),
     ]
     semaphores = [(21,), (16,), (2, 4, 2), (2, 4), (16,), (2, 4), (6,), (3,)]
-    semaphores += [(n,), (n,), (n, 2), (n, 2)] + [(n,)] * 4 + [(n // 2,), (n, 2), (n,)]
-    semaphores += [(3,), (3,), (4,), (4,), (4,), (3, 2), (5,), (5,)]
+    semaphores += [(n,), (n,), (n, 2), (n, 2)] + [(n,)] * 7
+    semaphores += [(3,), (3,), (4,), (4,), (4,), (3,), (1,), (5,), (5,)]
     return pl.pallas_call(
         layer_body,
         out_shape=(
             jax.ShapeDtypeStruct((n, 48, D), BF),
             jax.ShapeDtypeStruct((16, D), F32),
             jax.ShapeDtypeStruct(tok, BF),
-            jax.ShapeDtypeStruct((3, 2, BLOCK, D), BF),
+            jax.ShapeDtypeStruct(tok, BF),
         ),
         in_specs=[anywhere] * len(args),
         out_specs=[vmem] * 4,
@@ -830,16 +829,9 @@
 
 def finish_body(sums, vec, lay, parts, *outs):
     p = lax.rem(lax.axis_index("batch"), 8)
-    c = lax.rem(p, 2)
     layer_out, input_grad, g_q, g_k, g_v, g_o, g_inner, g_outer, b_inner = outs[:9]
     layer_out[...] = lay[...]
-    input_grad[...] = parts[:, 0]
-
-    @pl.when(c == 1)
-    def _():
-        for slot in range(1, 3):
-            both = parts[slot, 0].astype(F32) + parts[slot, 1].astype(F32)
-            input_grad[slot] = both.astype(BF)
+    input_grad[...] = parts[...]
 
     def piece(i):
         return sums[2 * i : 2 * i + 2].reshape(96, D).astype(F32)

time: 141 us -> 135 us (0.957); the launches traced: 141 us -> 133 us
  Pallas kernels: 140 us -> 132 us
    pallas_call x1, Pallas kernels: 135 us -> 128 us  [whole_layer(): pl.pallas_call(layer_body, out_shape=(jax.ShapeDtypeStruct((n, 48, D), BF...]
where the time goes in v5:
time: 135 us; the launch traced here: 133 us
  Pallas kernels  132 us (98%)
    pallas_call x1, Pallas kernels, whole_layer(): pl.pallas_call(layer_body, out_shape=(jax.ShapeDtypeStruct((n, 48, D), BF...  128 us
    pallas_call x1, Pallas kernels, finish(): pl.pallas_call(finish_body, out_shape=tuple((jax.ShapeDtypeStruct(s, t) f...  4.3 us

profile of v5, /device:TPU:0, one launch (start us, length us, event | category | flops | bytes accessed | tf_op | source)
XLA Modules:
  0.0 133.0 jit_solution(10260187019965458999)
XLA Ops:
  0.7 127.9 %shard_map.305 = (bf16[24,48,768]{2,1,0:T(8,128)(2,1)}, f32[16,768]{1,0:T(8,128)}, bf16[3,128,768]{2,1,0:T(8,128)(2,1)}, bf16[3,128,768]{2,1,0:T(8,128)(2,1)}) custom-call(bf16[3,2,64,768]{3,2,1,0:T(8,128)(2,1)} %bitcast.5, s32[3,128]{1,0:T(4,128)} %seg.1, bf16[3,128,768]{2,1,0:T(8,128)(2,1)} %cot.1, bf16[768,768]{1,0:T(8,128)(2,1)} %w_query_in.1, ...), custom_call_target="tpu_custom_call" | custom-call | tf_op jit(solution)/shard_map/pallas_call | solution.py:813
  128.6 4.3 %shard_map.306 = (bf16[3,128,768]{2,1,0:T(8,128)(2,1)}, bf16[3,128,768]{2,1,0:T(8,128)(2,1)}, f32[96,768]{1,0:T(8,128)}, f32[96,768]{1,0:T(8,128)}, f32[96,768]{...) custom-call(bf16[24,48,768]{2,1,0:T(8,128)(2,1)} %get-tuple-element., ...), custom_call_target="tpu_custom_call" | custom-call | tf_op jit(solution)/shard_map/pallas_call | solution.py:871

commit v6 on v5

--- a/solution.py
+++ b/solution.py
@@ -22,9 +22,9 @@
 CHUNKS = 24
 ORDER = "".join(
     (
-        "YBF2Y2F22YFF3233L23W342AA42534W24W325A43624535A42563A642565A",
-        "6354X6465W425663T32T2O3q3245T32k25346vV324655436245642563534",
-        "62465256345V64356364V546545V666VT",
+        "BYYYF22WF223F23WF23L2343A43A52243A45W4462352A53465A4365A6354",
+        "5X6426W4626T2352T23Oq34T5232k5v3644653265243V45356V354622645",
+        "6V56T24324V3654635354654656456V66",
     )
 )
 KINDS = "23456BFLAXTWOqkvYV"
@@ -165,8 +165,11 @@
     gain_second_in,
     shift_second_in,
     b_inner_in,
+    sums_hbm,
+    vec_hbm,
+    lay_hbm,
+    grad_hbm,
     sums,
-    vec_out,
     lay_out,
     grad_parts,
     pool,
@@ -231,6 +234,7 @@
     pr,
     vs,
     vr,
+    out_sem,
 ):
     z, beta, c, base = place()
     low = lane_low()
@@ -731,6 +735,16 @@
         rest = rest[last_turn + 1 :]
     emit(rest)
 
+    writes = []
+
+    def write(src, dst):
+        writes.append(pltpu.make_async_copy(src, dst, out_sem.at[len(writes)]))
+        writes[-1].start()
+
+    for slot in range(3):
+        layer_unit(slot).finish()
+        landed(lay_out.at[slot], lay_r.at[slot])
+    write(lay_out, lay_hbm)
     for i in range(CHUNKS):
         first_send(i).wait_send()
         for e in range(2):
@@ -747,8 +761,11 @@
             final_near(i).wait_send()
             cross_send(i).wait_send()
 
+        write(sums.at[i], sums_hbm.at[i])
+
     landed(rv.at[4], vr.at[4])
-    vec_out[...] = sv[4] + rv[4]
+    vec[...] = sv[4] + rv[4]
+    write(vec, vec_hbm)
     for i in range(5):
         vec_send(i).wait_send()
     for e in range(4):
@@ -757,21 +774,25 @@
     for n in (0, 1, 3):
         grad_unit(n).finish()
     for slot in range(3):
-        layer_unit(slot).finish()
-        landed(lay_out.at[slot], lay_r.at[slot])
         landed(grad_parts.at[slot], gr.at[slot])
+    write(grad_parts, grad_hbm)
+    for copy in writes:
+        copy.wait()
 
     move.finish()
 
 
 def whole_layer(tokens, segments, cotangent, weights, vectors):
-    vmem, anywhere = pl.BlockSpec(memory_space=pltpu.VMEM), pl.BlockSpec(memory_space=pl.ANY)
+    anywhere = pl.BlockSpec(memory_space=pl.ANY)
     dma = pltpu.SemaphoreType.DMA
     args = (tokens, segments, cotangent) + weights + vectors
     n = CHUNKS
     tok = (3, BLOCK, D)
     square = (16, 48, D)
     buffers = [
+        ((n, 48, D), BF),
+        (tok, BF),
+        (tok, BF),
         ((EARLY + FFN,) + square, BF),
         ((FFN,) + square, BF),
         ((D, D), BF),
@@ -809,7 +830,7 @@
     ]
     semaphores = [(21,), (16,), (2, 4, 2), (2, 4), (16,), (2, 4), (6,), (3,)]
     semaphores += [(n,), (n,), (n, 2), (n, 2)] + [(n,)] * 7
-    semaphores += [(3,), (3,), (4,), (4,), (4,), (3,), (1,), (5,), (5,)]
+    semaphores += [(3,), (3,), (4,), (4,), (4,), (3,), (1,), (5,), (5,), (n + 3,)]
     return pl.pallas_call(
         layer_body,
         out_shape=(
@@ -819,7 +840,7 @@
             jax.ShapeDtypeStruct(tok, BF),
         ),
         in_specs=[anywhere] * len(args),
-        out_specs=[vmem] * 4,
+        out_specs=[anywhere] * 4,
         scratch_shapes=[pltpu.VMEM(s, t) for s, t in buffers] + [dma(s) for s in semaphores],
         compiler_params=pltpu.CompilerParams(
             collective_id=0, has_side_effects=True, vmem_limit_bytes=int(63.9 * MIB)

time: 135 us -> 134 us (level); the launches traced: 133 us -> 134 us
  no operation moved by 1% of the time
where the time goes in v6:
time: 134 us
  Pallas kernels  133 us (99%)
    pallas_call x1, Pallas kernels, whole_layer(): pl.pallas_call(layer_body, out_shape=(jax.ShapeDtypeStruct((n, 48, D), BF...  129 us
    pallas_call x1, Pallas kernels, finish(): pl.pallas_call(finish_body, out_shape=tuple((jax.ShapeDtypeStruct(s, t) f...  4.3 us

profile of v6, /device:TPU:0, one launch (start us, length us, event | category | flops | bytes accessed | tf_op | source)
XLA Modules:
  0.0 133.7 jit_solution(14759994931028380498)
XLA Ops:
  0.7 128.5 %shard_map.305 = (bf16[24,48,768]{2,1,0:T(8,128)(2,1)}, f32[16,768]{1,0:T(8,128)}, bf16[3,128,768]{2,1,0:T(8,128)(2,1)}, bf16[3,128,768]{2,1,0:T(8,128)(2,1)}) custom-call(bf16[3,2,64,768]{3,2,1,0:T(8,128)(2,1)} %bitcast.5, s32[3,128]{1,0:T(4,128)} %seg.1, bf16[3,128,768]{2,1,0:T(8,128)(2,1)} %cot.1, bf16[768,768]{1,0:T(8,128)(2,1)} %w_query_in.1, ...), custom_call_target="tpu_custom_call" | custom-call | tf_op jit(solution)/shard_map/pallas_call | solution.py:834
  129.2 4.3 %shard_map.306 = (bf16[3,128,768]{2,1,0:T(8,128)(2,1)}, bf16[3,128,768]{2,1,0:T(8,128)(2,1)}, f32[96,768]{1,0:T(8,128)}, f32[96,768]{1,0:T(8,128)}, f32[96,768]{...) custom-call(bf16[24,48,768]{2,1,0:T(8,128)(2,1)} %get-tuple-element., ...), custom_call_target="tpu_custom_call" | custom-call | tf_op jit(solution)/shard_map/pallas_call | solution.py:892

commit v7 on v6

--- a/solution.py
+++ b/solution.py
@@ -22,9 +22,9 @@
 CHUNKS = 24
 ORDER = "".join(
     (
-        "BYYYF22WF223F23WF23L2343A43A52243A45W4462352A53465A4365A6354",
-        "5X6426W4626T2352T23Oq34T5232k5v3644653265243V45356V354622645",
-        "6V56T24324V3654635354654656456V66",
+        "BFYY2Y2F22F3W2F23W33L3242A4A54342A3542W5346A524635A3645A5364",
+        "2625X546W4626T36232T5O34q323254T25k263v26534424T6535534V6343",
+        "456V2652465463V5654356646545V66V6",
     )
 )
 KINDS = "23456BFLAXTWOqkvYV"
@@ -382,8 +382,9 @@
     lse[...] = jnp.zeros_like(lse)
     project(0)
     attend(0, (0, 1), 0, PAIRS)
-    forward_rows(1)
+    forward_rows(1, range(3))
     send_cotangents()
+    forward_rows(1, range(3, 4))
     got_out.wait()
     out_norm((0, 1))
     project(1)

time: 134 us -> 133 us (level)
  no operation moved by 1% of the time
where the time goes in v7:
time: 133 us
  Pallas kernels  132 us (99%)
    pallas_call x1, Pallas kernels, whole_layer(): pl.pallas_call(layer_body, out_shape=(jax.ShapeDtypeStruct((n, 48, D), BF...  128 us
    pallas_call x1, Pallas kernels, finish(): pl.pallas_call(finish_body, out_shape=tuple((jax.ShapeDtypeStruct(s, t) f...  4.3 us

profile of v7, /device:TPU:0, one launch (start us, length us, event | category | flops | bytes accessed | tf_op | source)
XLA Modules:
  0.0 133.3 jit_solution(13540011914890547085)
XLA Ops:
  0.7 128.1 %shard_map.305 = (bf16[24,48,768]{2,1,0:T(8,128)(2,1)}, f32[16,768]{1,0:T(8,128)}, bf16[3,128,768]{2,1,0:T(8,128)(2,1)}, bf16[3,128,768]{2,1,0:T(8,128)(2,1)}) custom-call(bf16[3,2,64,768]{3,2,1,0:T(8,128)(2,1)} %bitcast.5, s32[3,128]{1,0:T(4,128)} %seg.1, bf16[3,128,768]{2,1,0:T(8,128)(2,1)} %cot.1, bf16[768,768]{1,0:T(8,128)(2,1)} %w_query_in.1, ...), custom_call_target="tpu_custom_call" | custom-call | tf_op jit(solution)/shard_map/pallas_call | solution.py:835
  128.8 4.3 %shard_map.306 = (bf16[3,128,768]{2,1,0:T(8,128)(2,1)}, bf16[3,128,768]{2,1,0:T(8,128)(2,1)}, f32[96,768]{1,0:T(8,128)}, f32[96,768]{1,0:T(8,128)}, f32[96,768]{...) custom-call(bf16[24,48,768]{2,1,0:T(8,128)(2,1)} %get-tuple-element., ...), custom_call_target="tpu_custom_call" | custom-call | tf_op jit(solution)/shard_map/pallas_call | solution.py:893
